TPU v7x, 32 devices: a whole 2x2x4 slice. The times are simulated.
32 devices in a mesh: slot: 2 (over y), ctx: 4 (over z), fsdp: 4 (over x, core).
Axes of the slice: x: 2, y: 2, z: 4, core: 2. Of those that a mesh axis runs over, the one named last changes fastest.
Arguments:
- tokens: bfloat16 [4, 2048, 1024], P('slot', ('ctx', 'fsdp')), may hold values from -6 to 6
- lengths: int32 [4], P('slot'), may hold values from 1024 to 2048, as said below
- w_qkv: bfloat16 [1024, 3072], P(('ctx', 'fsdp')), may hold values from -0.25 to 0.25
- b_qkv: bfloat16 [3072], P(('ctx', 'fsdp')), may hold values from -1.796875 to 1.796875
- w_out: bfloat16 [1024, 1024], P(('ctx', 'fsdp')), may hold values from -1.5 to 1.5
- b_out: bfloat16 [1024], P(('ctx', 'fsdp')), may hold values from -1.796875 to 1.796875
- ln1_gain: bfloat16 [1024], P(('ctx', 'fsdp')), may hold values from 0.5 to 1.5
- ln1_bias: bfloat16 [1024], P(('ctx', 'fsdp')), may hold values from -1.796875 to 1.796875
- w_up: bfloat16 [1024, 4096], P(('ctx', 'fsdp')), may hold values from -0.1875 to 0.1875
- b_up: bfloat16 [4096], P(('ctx', 'fsdp')), may hold values from -1.796875 to 1.796875
- w_down: bfloat16 [4096, 1024], P(('ctx', 'fsdp')), may hold values from -0.09375 to 0.09375
- b_down: bfloat16 [1024], P(('ctx', 'fsdp')), may hold values from -1.796875 to 1.796875
- ln2_gain: bfloat16 [1024], P(('ctx', 'fsdp')), may hold values from 0.5 to 1.5
- ln2_bias: bfloat16 [1024], P(('ctx', 'fsdp')), may hold values from -1.796875 to 1.796875
- w_proj: bfloat16 [1024, 128], P(('ctx', 'fsdp')), may hold values from -0.1875 to 0.1875
- cot_out: bfloat16 [4, 2048, 1024], P('slot', ('ctx', 'fsdp')), may hold values from -6 to 6
- cot_emb: bfloat16 [4, 2048, 128], P('slot', ('ctx', 'fsdp')), may hold values from -6 to 6
Outputs:
- layer_out: bfloat16 [4, 2048, 1024], P('slot', ('ctx', 'fsdp'))
- embeds: bfloat16 [4, 2048, 128], P('slot', ('ctx', 'fsdp'))
- input_grad: bfloat16 [4, 2048, 1024], P('slot', ('ctx', 'fsdp'))
- grad_w_qkv: float32 [1024, 3072], P(('ctx', 'fsdp'))
- grad_b_qkv: float32 [3072], P(('ctx', 'fsdp'))
- grad_w_out: float32 [1024, 1024], P(('ctx', 'fsdp'))
- grad_b_out: float32 [1024], P(('ctx', 'fsdp'))
- grad_ln1_gain: float32 [1024], P(('ctx', 'fsdp'))
- grad_ln1_bias: float32 [1024], P(('ctx', 'fsdp'))
- grad_w_up: float32 [1024, 4096], P(('ctx', 'fsdp'))
- grad_b_up: float32 [4096], P(('ctx', 'fsdp'))
- grad_w_down: float32 [4096, 1024], P(('ctx', 'fsdp'))
- grad_b_down: float32 [1024], P(('ctx', 'fsdp'))
- grad_ln2_gain: float32 [1024], P(('ctx', 'fsdp'))
- grad_ln2_bias: float32 [1024], P(('ctx', 'fsdp'))
- grad_w_proj: float32 [1024, 128], P(('ctx', 'fsdp'))
Inputs may be any that keep to these rules, and one draw needn't show every extreme that they name: Each slot holds lengths valid positions at its start; in every draw some slot is full (2048) and some slot holds exactly 1024.
All inputs are finite; a program needn't handle non-finite values.
Results may differ from a plain program's by a relative error of at most 0.018.
Values may be sent and summed in bfloat16 or wider, within the bound.
A program may use at most 192 MiB of HBM per device.

v0:
```python
from functools import partial

import jax
import jax.numpy as jnp
from jax import lax
from jax.sharding import PartitionSpec as P

H = 16
HD = 64


NEG_FILL = -1e30
LN_EPS = 1e-05


def layer_norm(hidden, gain, shift):
    center = hidden - jnp.mean(hidden, axis=-1, keepdims=True)
    spread = jnp.mean(center * center, axis=-1, keepdims=True)
    return center * lax.rsqrt(spread + LN_EPS) * gain + shift


def rope_tables(positions, head_width):
    halfway = head_width // 2
    ladder = jnp.arange(halfway, dtype=jnp.float32) * (2.0 / head_width)
    frequency = jnp.power(jnp.float32(10000.0), -ladder)
    angles = positions[:, None] * frequency[None, :]
    return (jnp.cos(angles)[:, None, :], jnp.sin(angles)[:, None, :])


def rotate(values, cosine, sine_part):
    halfway = values.shape[-1] // 2
    first_half = values[..., :halfway]
    second_half = values[..., halfway:]
    return jnp.concatenate(
        [
            first_half * cosine - second_half * sine_part,
            second_half * cosine + first_half * sine_part,
        ],
        axis=-1,
    )


def block_scores(query_block, key_block, key_start, length, scale):
    scores = (
        jnp.einsum("qhd,khd->hqk", query_block, key_block, preferred_element_type=jnp.float32)
        * scale
    )
    key_ids = key_start + jnp.arange(key_block.shape[0], dtype=jnp.int32)
    return jnp.where((key_ids < length)[None, None, :], scores, NEG_FILL)


def per_device(
    tokens,
    lengths,
    w_qkv,
    b_qkv,
    w_out,
    b_out,
    ln1_gain,
    ln1_bias,
    w_up,
    b_up,
    w_down,
    b_down,
    ln2_gain,
    ln2_bias,
    w_proj,
    cot_out,
    cot_emb,
):
    n_fsdp = lax.axis_size("fsdp")
    n_ctx = lax.axis_size("ctx")
    ctx_at = lax.axis_index("ctx")
    fsdp_at = lax.axis_index("fsdp")
    groups, tok_slot, width = tokens.shape
    heads_here = H // n_fsdp
    lane_width = heads_here * HD
    span_rows = tok_slot * n_fsdp
    key_count = span_rows * n_ctx
    row_count = groups * tok_slot
    scale = HD ** (-0.5)
    query_rows = min(512, span_rows)
    key_rows = min(2048, key_count // 4)
    query_blocks = span_rows // query_rows
    key_blocks = key_count // key_rows
    key_starts = jnp.arange(key_blocks, dtype=jnp.int32) * key_rows
    qkv_full, qkv_bias, out_full, out_bias, gain_one, shift_one = (
        lax.all_gather(w_qkv, ("ctx", "fsdp"), axis=0, tiled=True),
        lax.all_gather(b_qkv, ("ctx", "fsdp"), axis=0, tiled=True),
        lax.all_gather(w_out, ("ctx", "fsdp"), axis=0, tiled=True),
        lax.all_gather(b_out, ("ctx", "fsdp"), axis=0, tiled=True),
        lax.all_gather(ln1_gain, ("ctx", "fsdp"), axis=0, tiled=True),
        lax.all_gather(ln1_bias, ("ctx", "fsdp"), axis=0, tiled=True),
    )
    token_pos = (ctx_at * n_fsdp + fsdp_at) * tok_slot + jnp.arange(tok_slot, dtype=jnp.int32)
    live_rows = (token_pos[None, :] < lengths[:, None]).reshape(row_count, 1)
    flat_tokens = tokens.reshape(row_count, width)
    joined = jnp.dot(flat_tokens, qkv_full, preferred_element_type=jnp.float32) + qkv_bias.astype(
        jnp.float32
    )
    cosine, sine_part = rope_tables(token_pos.astype(jnp.float32), HD)
    split_heads = joined.reshape(groups, tok_slot, 3, H, HD)
    rotated_query = rotate(split_heads[:, :, 0], cosine, sine_part)
    rotated_key = rotate(split_heads[:, :, 1], cosine, sine_part)
    packed = (
        jnp.stack([rotated_query, rotated_key, split_heads[:, :, 2]], axis=2)
        .astype(jnp.bfloat16)
        .reshape(groups, tok_slot, 3, n_fsdp, lane_width)
    )
    by_heads = lax.all_to_all(packed, "fsdp", split_axis=3, concat_axis=1, tiled=True)
    queries = by_heads[:, :, 0, 0]
    local_keys = by_heads[:, :, 1, 0]
    local_values = by_heads[:, :, 2, 0]
    all_keys, all_values = (
        lax.all_gather(local_keys, "ctx", axis=1, tiled=True),
        lax.all_gather(local_values, "ctx", axis=1, tiled=True),
    )

    def attend_slot(slot_item):
        slot_queries, slot_keys, slot_values, length = slot_item
        query_split = slot_queries.reshape(query_blocks, query_rows, heads_here, HD)
        key_split = slot_keys.reshape(key_blocks, key_rows, heads_here, HD)
        value_split = slot_values.reshape(key_blocks, key_rows, heads_here, HD)

        def per_query(query_block):

            def row_stats(state_pair, key_item):
                highest, running_sum = state_pair
                scores = block_scores(query_block, key_item[0], key_item[1], length, scale)
                new_high = jnp.maximum(highest, jnp.max(scores, axis=-1))
                running_sum = running_sum * jnp.exp(highest - new_high) + jnp.sum(
                    jnp.exp(scores - new_high[..., None]), axis=-1
                )
                return ((new_high, running_sum), None)

            start_state = (
                jnp.full((heads_here, query_rows), NEG_FILL, jnp.float32),
                jnp.zeros((heads_here, query_rows), jnp.float32),
            )
            highest, running_sum = lax.scan(row_stats, start_state, (key_split, key_starts))[0]
            log_norm = highest + jnp.log(running_sum)

            def weigh_values(accumulated, key_item):
                scores = block_scores(query_block, key_item[0], key_item[2], length, scale)
                weights = jnp.exp(scores - log_norm[..., None]).astype(jnp.bfloat16)
                return (
                    accumulated
                    + jnp.einsum(
                        "hqk,khd->qhd", weights, key_item[1], preferred_element_type=jnp.float32
                    ),
                    None,
                )

            mixture = lax.scan(
                weigh_values,
                jnp.zeros((query_rows, heads_here, HD), jnp.float32),
                (key_split, value_split, key_starts),
            )[0]
            return (mixture, log_norm)

        mixture, log_norm = lax.map(per_query, query_split)
        return (mixture.reshape(span_rows, lane_width), log_norm)

    mixture, log_norms = lax.map(attend_slot, (queries, all_keys, all_values, lengths))
    merged = lax.all_to_all(
        mixture.astype(jnp.bfloat16).reshape(groups, span_rows, 1, lane_width),
        "fsdp",
        split_axis=1,
        concat_axis=2,
        tiled=True,
    ).reshape(row_count, width)
    attended = jnp.dot(merged, out_full, preferred_element_type=jnp.float32) + out_bias.astype(
        jnp.float32
    )
    hidden_one, pull_one = jax.vjp(
        layer_norm,
        flat_tokens.astype(jnp.float32) + attended,
        gain_one.astype(jnp.float32),
        shift_one.astype(jnp.float32),
    )
    hidden_low = hidden_one.astype(jnp.bfloat16)
    up_full, up_bias, down_full, down_bias, gain_two, shift_two, proj_full = (
        lax.all_gather(w_up, ("ctx", "fsdp"), axis=0, tiled=True),
        lax.all_gather(b_up, ("ctx", "fsdp"), axis=0, tiled=True),
        lax.all_gather(w_down, ("ctx", "fsdp"), axis=0, tiled=True),
        lax.all_gather(b_down, ("ctx", "fsdp"), axis=0, tiled=True),
        lax.all_gather(ln2_gain, ("ctx", "fsdp"), axis=0, tiled=True),
        lax.all_gather(ln2_bias, ("ctx", "fsdp"), axis=0, tiled=True),
        lax.all_gather(w_proj, ("ctx", "fsdp"), axis=0, tiled=True),
    )
    upward = jnp.dot(hidden_low, up_full, preferred_element_type=jnp.float32) + up_bias.astype(
        jnp.float32
    )
    active_full, pull_gelu = jax.vjp(partial(jax.nn.gelu, approximate=False), upward)
    active = active_full.astype(jnp.bfloat16)
    downward = jnp.dot(active, down_full, preferred_element_type=jnp.float32) + down_bias.astype(
        jnp.float32
    )
    out_full_rows, pull_two = jax.vjp(
        layer_norm,
        hidden_one + downward,
        gain_two.astype(jnp.float32),
        shift_two.astype(jnp.float32),
    )
    out_low = out_full_rows.astype(jnp.bfloat16)
    projected = jnp.dot(out_low, proj_full, preferred_element_type=jnp.float32)
    back_qkv, back_qkv_bias, back_out, back_out_bias, back_gain_one, back_shift_one = (
        lax.all_gather(w_qkv, ("ctx", "fsdp"), axis=0, tiled=True),
        lax.all_gather(b_qkv, ("ctx", "fsdp"), axis=0, tiled=True),
        lax.all_gather(w_out, ("ctx", "fsdp"), axis=0, tiled=True),
        lax.all_gather(b_out, ("ctx", "fsdp"), axis=0, tiled=True),
        lax.all_gather(ln1_gain, ("ctx", "fsdp"), axis=0, tiled=True),
        lax.all_gather(ln1_bias, ("ctx", "fsdp"), axis=0, tiled=True),
    )
    back_up, back_up_bias, back_down, back_down_bias, back_gain_two, back_shift_two, back_proj = (
        lax.all_gather(w_up, ("ctx", "fsdp"), axis=0, tiled=True),
        lax.all_gather(b_up, ("ctx", "fsdp"), axis=0, tiled=True),
        lax.all_gather(w_down, ("ctx", "fsdp"), axis=0, tiled=True),
        lax.all_gather(b_down, ("ctx", "fsdp"), axis=0, tiled=True),
        lax.all_gather(ln2_gain, ("ctx", "fsdp"), axis=0, tiled=True),
        lax.all_gather(ln2_bias, ("ctx", "fsdp"), axis=0, tiled=True),
        lax.all_gather(w_proj, ("ctx", "fsdp"), axis=0, tiled=True),
    )
    grad_out = jnp.where(live_rows, cot_out.reshape(row_count, width).astype(jnp.float32), 0.0)
    grad_emb = jnp.where(live_rows, cot_emb.reshape(row_count, -1), 0)
    d_proj = jnp.einsum("rd,rp->dp", out_low, grad_emb, preferred_element_type=jnp.float32)
    grad_full = grad_out + jnp.einsum(
        "rp,dp->rd", grad_emb, back_proj, preferred_element_type=jnp.float32
    )
    grad_two, d_gain_two, d_shift_two = pull_two(grad_full)
    grad_down = grad_two.astype(jnp.bfloat16)
    d_down = jnp.einsum("rf,rd->fd", active, grad_down, preferred_element_type=jnp.float32)
    d_down_bias = jnp.sum(grad_down.astype(jnp.float32), axis=0)
    grad_act = jnp.einsum("rd,fd->rf", grad_down, back_down, preferred_element_type=jnp.float32)
    grad_up = pull_gelu(grad_act)[0].astype(jnp.bfloat16)
    d_up = jnp.einsum("rd,rf->df", hidden_low, grad_up, preferred_element_type=jnp.float32)
    d_up_bias = jnp.sum(grad_up.astype(jnp.float32), axis=0)
    grad_hidden = grad_two + jnp.einsum(
        "rf,df->rd", grad_up, back_up, preferred_element_type=jnp.float32
    )
    grad_one, d_gain_one, d_shift_one = pull_one(grad_hidden)
    grad_att = grad_one.astype(jnp.bfloat16)
    d_out = jnp.einsum("rd,re->de", merged, grad_att, preferred_element_type=jnp.float32)
    d_out_bias = jnp.sum(grad_att.astype(jnp.float32), axis=0)
    grad_merged = jnp.einsum(
        "re,de->rd", grad_att, back_out, preferred_element_type=jnp.float32
    ).astype(jnp.bfloat16)
    grad_heads = lax.all_to_all(
        grad_merged.reshape(groups, tok_slot, n_fsdp, lane_width),
        "fsdp",
        split_axis=2,
        concat_axis=1,
        tiled=True,
    ).reshape(groups, span_rows, lane_width)

    def attend_back(slot_item):
        slot_queries, slot_keys, slot_values, grad_mix, log_norm, length = slot_item
        query_split = slot_queries.reshape(query_blocks, query_rows, heads_here, HD)
        key_split = slot_keys.reshape(key_blocks, key_rows, heads_here, HD)
        value_split = slot_values.reshape(key_blocks, key_rows, heads_here, HD)
        grad_split = grad_mix.reshape(query_blocks, query_rows, heads_here, HD)

        def value_pass(value_total, query_item):
            query_block, grad_block, norm_block = query_item

            def value_per_key(row_dot, key_item):
                key_block, value_block, key_start = key_item
                scores = block_scores(query_block, key_block, key_start, length, scale)
                probability = jnp.exp(scores - norm_block[..., None])
                grad_probs = jnp.einsum(
                    "qhd,khd->hqk", grad_block, value_block, preferred_element_type=jnp.float32
                )
                value_part = jnp.einsum(
                    "hqk,qhd->khd",
                    probability.astype(jnp.bfloat16),
                    grad_block,
                    preferred_element_type=jnp.float32,
                )
                return (row_dot + jnp.sum(probability * grad_probs, axis=-1), value_part)

            row_dot, value_parts = lax.scan(
                value_per_key,
                jnp.zeros((heads_here, query_rows), jnp.float32),
                (key_split, value_split, key_starts),
            )
            return (value_total + value_parts.reshape(key_count, heads_here, HD), row_dot)

        value_grad, row_dots = lax.scan(
            value_pass,
            jnp.zeros((key_count, heads_here, HD), jnp.float32),
            (query_split, grad_split, log_norm),
        )

        def key_pass(key_total, query_item):
            query_block, grad_block, norm_block, dot_block = query_item

            def key_per_key(query_accum, key_item):
                key_block, value_block, key_start = key_item
                scores = block_scores(query_block, key_block, key_start, length, scale)
                probability = jnp.exp(scores - norm_block[..., None])
                grad_probs = jnp.einsum(
                    "qhd,khd->hqk", grad_block, value_block, preferred_element_type=jnp.float32
                )
                grad_scores = (probability * (grad_probs - dot_block[..., None])).astype(
                    jnp.bfloat16
                )
                query_accum = query_accum + jnp.einsum(
                    "hqk,khd->qhd", grad_scores, key_block, preferred_element_type=jnp.float32
                )
                key_part = jnp.einsum(
                    "hqk,qhd->khd", grad_scores, query_block, preferred_element_type=jnp.float32
                )
                return (query_accum, key_part)

            query_grad, key_parts = lax.scan(
                key_per_key,
                jnp.zeros((query_rows, heads_here, HD), jnp.float32),
                (key_split, value_split, key_starts),
            )
            return (key_total + key_parts.reshape(key_count, heads_here, HD), query_grad)

        key_grad, query_grads = lax.scan(
            key_pass,
            jnp.zeros((key_count, heads_here, HD), jnp.float32),
            (query_split, grad_split, log_norm, row_dots),
        )
        return (
            query_grads.reshape(span_rows, lane_width) * scale,
            key_grad.reshape(key_count, lane_width) * scale,
            value_grad.reshape(key_count, lane_width),
        )

    grad_queries, key_terms, value_terms = lax.map(
        attend_back, (queries, all_keys, all_values, grad_heads, log_norms, lengths)
    )
    grad_keys, grad_values = (
        lax.psum_scatter(
            key_terms.astype(jnp.bfloat16), "ctx", scatter_dimension=1, tiled=True
        ).astype(jnp.float32),
        lax.psum_scatter(
            value_terms.astype(jnp.bfloat16), "ctx", scatter_dimension=1, tiled=True
        ).astype(jnp.float32),
    )
    head_pos = (ctx_at * span_rows + jnp.arange(span_rows, dtype=jnp.int32)).astype(jnp.float32)
    head_cosine, head_sine = rope_tables(head_pos, HD)
    query_back = rotate(
        grad_queries.reshape(groups, span_rows, heads_here, HD), head_cosine, -head_sine
    )
    key_back = rotate(grad_keys.reshape(groups, span_rows, heads_here, HD), head_cosine, -head_sine)
    value_back = grad_values.reshape(groups, span_rows, heads_here, HD)
    grad_pack = (
        jnp.stack([query_back, key_back, value_back], axis=2)
        .astype(jnp.bfloat16)
        .reshape(groups, span_rows, 3, 1, lane_width)
    )
    grad_joined = lax.all_to_all(
        grad_pack, "fsdp", split_axis=1, concat_axis=3, tiled=True
    ).reshape(row_count, 3 * width)
    d_qkv = jnp.einsum("rd,re->de", flat_tokens, grad_joined, preferred_element_type=jnp.float32)
    d_qkv_bias = jnp.sum(grad_joined.astype(jnp.float32), axis=0)
    input_grad = (
        jnp.einsum("re,de->rd", grad_joined, back_qkv, preferred_element_type=jnp.float32)
        + grad_one
    ).astype(jnp.bfloat16)
    shards = (
        lax.psum_scatter(d_qkv, ("ctx", "fsdp"), scatter_dimension=0, tiled=True),
        lax.psum_scatter(d_qkv_bias, ("ctx", "fsdp"), scatter_dimension=0, tiled=True),
        lax.psum_scatter(d_out, ("ctx", "fsdp"), scatter_dimension=0, tiled=True),
        lax.psum_scatter(d_out_bias, ("ctx", "fsdp"), scatter_dimension=0, tiled=True),
        lax.psum_scatter(d_gain_one, ("ctx", "fsdp"), scatter_dimension=0, tiled=True),
        lax.psum_scatter(d_shift_one, ("ctx", "fsdp"), scatter_dimension=0, tiled=True),
        lax.psum_scatter(d_up, ("ctx", "fsdp"), scatter_dimension=0, tiled=True),
        lax.psum_scatter(d_up_bias, ("ctx", "fsdp"), scatter_dimension=0, tiled=True),
        lax.psum_scatter(d_down, ("ctx", "fsdp"), scatter_dimension=0, tiled=True),
        lax.psum_scatter(d_down_bias, ("ctx", "fsdp"), scatter_dimension=0, tiled=True),
        lax.psum_scatter(d_gain_two, ("ctx", "fsdp"), scatter_dimension=0, tiled=True),
        lax.psum_scatter(d_shift_two, ("ctx", "fsdp"), scatter_dimension=0, tiled=True),
        lax.psum_scatter(d_proj, ("ctx", "fsdp"), scatter_dimension=0, tiled=True),
    )
    totals = (
        lax.psum(shards[0].astype(jnp.bfloat16), "slot").astype(jnp.float32),
        lax.psum(shards[1].astype(jnp.bfloat16), "slot").astype(jnp.float32),
        lax.psum(shards[2].astype(jnp.bfloat16), "slot").astype(jnp.float32),
        lax.psum(shards[3].astype(jnp.bfloat16), "slot").astype(jnp.float32),
        lax.psum(shards[4].astype(jnp.bfloat16), "slot").astype(jnp.float32),
        lax.psum(shards[5].astype(jnp.bfloat16), "slot").astype(jnp.float32),
        lax.psum(shards[6].astype(jnp.bfloat16), "slot").astype(jnp.float32),
        lax.psum(shards[7].astype(jnp.bfloat16), "slot").astype(jnp.float32),
        lax.psum(shards[8].astype(jnp.bfloat16), "slot").astype(jnp.float32),
        lax.psum(shards[9].astype(jnp.bfloat16), "slot").astype(jnp.float32),
        lax.psum(shards[10].astype(jnp.bfloat16), "slot").astype(jnp.float32),
        lax.psum(shards[11].astype(jnp.bfloat16), "slot").astype(jnp.float32),
        lax.psum(shards[12].astype(jnp.bfloat16), "slot").astype(jnp.float32),
    )
    return (
        out_low.reshape(groups, tok_slot, width),
        projected.astype(jnp.bfloat16).reshape(groups, tok_slot, -1),
        input_grad.reshape(groups, tok_slot, width),
        totals[0],
        totals[1],
        totals[2],
        totals[3],
        totals[4],
        totals[5],
        totals[6],
        totals[7],
        totals[8],
        totals[9],
        totals[10],
        totals[11],
        totals[12],
    )


def solution(mesh):
    in_specs = (
        P("slot", ("ctx", "fsdp"), None),
        P("slot"),
        P(("ctx", "fsdp"), None),
        P(("ctx", "fsdp")),
        P(("ctx", "fsdp"), None),
        P(("ctx", "fsdp")),
        P(("ctx", "fsdp")),
        P(("ctx", "fsdp")),
        P(("ctx", "fsdp"), None),
        P(("ctx", "fsdp")),
        P(("ctx", "fsdp"), None),
        P(("ctx", "fsdp")),
        P(("ctx", "fsdp")),
        P(("ctx", "fsdp")),
        P(("ctx", "fsdp"), None),
        P("slot", ("ctx", "fsdp"), None),
        P("slot", ("ctx", "fsdp"), None),
    )
    out_specs = (
        P("slot", ("ctx", "fsdp"), None),
        P("slot", ("ctx", "fsdp"), None),
        P("slot", ("ctx", "fsdp"), None),
        P(("ctx", "fsdp"), None),
        P(("ctx", "fsdp")),
        P(("ctx", "fsdp"), None),
        P(("ctx", "fsdp")),
        P(("ctx", "fsdp")),
        P(("ctx", "fsdp")),
        P(("ctx", "fsdp"), None),
        P(("ctx", "fsdp")),
        P(("ctx", "fsdp"), None),
        P(("ctx", "fsdp")),
        P(("ctx", "fsdp")),
        P(("ctx", "fsdp")),
        P(("ctx", "fsdp"), None),
    )
    return jax.shard_map(
        per_device, mesh=mesh, in_specs=in_specs, out_specs=out_specs, check_vma=False
    )
```

profile of v0, /device:TPU:0, one launch (start us, length us, event | category | flops | bytes accessed | tf_op | source)
XLA Modules:
  0.0 1485.3 jit_solution(5087836077966394685)
XLA Ops:
  16.5 65.1 %all-reduce.16 = (bf16[3072]{0:T(1024)(128)(2,1)S(1)}, bf16[1024]{0:T(1024)(128)(2,1)S(1)}, bf16[1024]{0:T(1024)(128)(2,1)S(1)}, bf16[1024]{0:T(1024)(128)(2,1)S...) all-reduce(bf16[3072]{0:T(1024)(128)(2,1)S(1)} %dynamic-update-slic, ...), channel_id=1, replica_groups=mesh['slot'=2,'ctx'=4,'fsdp'=4] {'ctx','fsdp'}, use_global_device_ids=true, to_apply=%add | all-reduce | flops 9216 | bytes 36864
  82.1 6.4 convolution_add_fusion.1
  100.5 22.5 %all_to_all.63 = bf16[2,128,3,4,256]{1,4,0,2,3:T(8,128)(2,1)S(1)} all-to-all(bf16[2,128,3,4,256]{1,4,0,2,3:T(8,128)(2,1)S(1)} %copy.134), channel_id=1, replica_groups=mesh['slot'=2,'ctx'=4,'fsdp'=4] {'fsdp'}, dimensions={3} | all-to-all | bytes 3145728 | tf_op jit(solution)/shard_map/all_to_all | solution.py:110
  128.4 39.5 %all-gather.18.cloned.1.call-done = bf16[2,2048,1,1,256]{4,1,2,0,3:T(8,128)(2,1)} async-done(((bf16[2,512,1,1,256]{4,1,2,0,3:T(8,128)(2,1)}), bf16[2,2048,1,1,256]{4,1,2,0,3:T(8,128)(2,1)}) %all-gather.18.cloned.1.call-update) | async-done | bytes 2097168 | tf_op jit(solution)/shard_map/all_gather | solution.py:115
  167.9 4.0 copy.136
  171.9 42.7 %all-gather.20.cloned.1.call-done = bf16[2,2048,1,1,256]{4,1,2,0,3:T(8,128)(2,1)} async-done(((bf16[2,512,1,1,256]{4,1,2,0,3:T(8,128)(2,1)}), bf16[2,2048,1,1,256]{4,1,2,0,3:T(8,128)(2,1)}) %all-gather.20.cloned.1.call-update) | async-done | bytes 2097168 | tf_op jit(solution)/shard_map/all_gather | solution.py:116
  214.5 4.0 copy.137
  218.5 129.3 %while.120 = (s32[]{:T(128)}, bf16[2,512,256]{2,0,1:T(2,128)(2,1)}, f32[2,1,4,512]{3,2,1,0:T(4,128)S(1)}, bf16[2,2048,256]{1,2,0:T(8,128)(2,1)}, bf16[2,2048,256...) while((s32[]{:T(128)}, bf16[2,512,256]{2,0,1:T(2,128)(2,1)}, ...), condition=%wide.region_7.8_spmd.clone.clone, body=%wide.region_0.7_spmd.clone.clone.sunk | while | flops 414464000 | bytes 29511820 | solution.py:164
  222.8 32.0 %while.124 = (s32[]{:T(128)}, f32[4,512]{1,0:T(4,128)S(1)}, f32[4,512]{1,0:T(4,128)S(1)}, s32[4]{0:T(128)S(1)}, s32[]{:T(128)}, /*index=5*/bf16[4,512,4,64]{1,3,...) while((s32[]{:T(128)}, f32[4,512]{1,0:T(4,128)S(1)}, ...), condition=%wide.region_4.4_spmd.clone, body=%wide.region_1.3_spmd.clone.sunk | while | flops 141569024 | bytes 9021056 | solution.py:140
  256.0 18.6 %while.125 = (s32[]{:T(128)}, f32[512,4,64]{0,2,1:T(8,128)S(1)}, bf16[4,512,4,64]{1,3,2,0:T(8,128)(2,1)S(1)}, s32[4]{0:T(128)S(1)}, s32[]{:T(128)}, /*index=5*/b...) while((s32[]{:T(128)}, f32[512,4,64]{0,2,1:T(8,128)S(1)}, ...), condition=%wide.region_6.6_spmd.clone, body=%wide.region_5.5_spmd.clone.sunk | while | flops 272892928 | bytes 1845379 | solution.py:154
  275.1 6.9 dynamic_update_slice.59
  287.1 32.7 %while.124 = (s32[]{:T(128)}, f32[4,512]{1,0:T(4,128)S(1)}, f32[4,512]{1,0:T(4,128)S(1)}, s32[4]{0:T(128)S(1)}, s32[]{:T(128)}, /*index=5*/bf16[4,512,4,64]{1,3,...) while((s32[]{:T(128)}, f32[4,512]{1,0:T(4,128)S(1)}, ...), condition=%wide.region_4.4_spmd.clone, body=%wide.region_1.3_spmd.clone.sunk | while | flops 141569024 | bytes 9021056 | solution.py:140
  320.9 18.6 %while.125 = (s32[]{:T(128)}, f32[512,4,64]{0,2,1:T(8,128)S(1)}, bf16[4,512,4,64]{1,3,2,0:T(8,128)(2,1)S(1)}, s32[4]{0:T(128)S(1)}, s32[]{:T(128)}, /*index=5*/b...) while((s32[]{:T(128)}, f32[512,4,64]{0,2,1:T(8,128)S(1)}, ...), condition=%wide.region_6.6_spmd.clone, body=%wide.region_5.5_spmd.clone.sunk | while | flops 272892928 | bytes 1845379 | solution.py:154
  340.1 6.9 dynamic_update_slice.59
  351.4 20.0 %all-gather.2 = bf16[16,1,256]{2,1,0:T(2,128)(2,1)S(1)} all-gather(bf16[1,1,256]{2,1,0:T(2,128)(2,1)S(1)} %reshape.490), channel_id=1, replica_groups=mesh['slot'=2,'ctx'=4,'fsdp'=4] {'ctx','fsdp'}, dimensions={0}, use_global_device_ids=true | all-gather | bytes 8704 | tf_op jit(solution)/shard_map/all_gather | solution.py:184
  371.5 20.8 %all_gather.64 = bf16[1024,128]{1,0:T(8,128)(2,1)S(1)} all-gather(bf16[64,128]{1,0:T(8,128)(2,1)S(1)} %copy-done.34), channel_id=1, replica_groups=mesh['slot'=2,'ctx'=4,'fsdp'=4] {'ctx','fsdp'}, dimensions={0}, use_global_device_ids=true | all-gather | bytes 278528 | tf_op jit(solution)/shard_map/all_gather | solution.py:189
  396.2 16.5 %multiply_convert_fusion.1 = (bf16[256,4096]{1,0:T(8,128)(2,1)}, f32[256,4096]{1,0:T(8,128)}, f32[256,4096]{1,0:T(8,128)}) fusion(f32[4096]{0:T(1024)S(1)} %bitcast.285, bf16[1024,4096]{1,0:T(8,128)(2,1)} %all-gather.14.cloned.1.call-done, f32[256,1024]{1,0:T(8,128)S(1)} %get-tuple-element.1152, f32[1024]{0:T(1024)S(1)} %convert_element_type.201, ...), kind=kOutput, calls=%fused_computation.83 | convolution fusion | flops 2218000384 | bytes 19949568 | tf_op jit(solution)/shard_map/dot_general | solution.py:191
  412.7 6.5 fusion.74
  423.2 6.9 convert_reduce_fusion
  430.1 7.5 multiply_reduce_fusion.2
  446.1 8.7 all-to-all-done.2
  455.6 215.6 %while.123 = (s32[]{:T(128)}, f32[2,512,256]{1,2,0:T(8,128)}, bf16[2,2048,256]{1,2,0:T(8,128)(2,1)}, bf16[2,2048,256]{1,2,0:T(8,128)(2,1)}, bf16[2,2048,256]{1,2...) while((s32[]{:T(128)}, f32[2,512,256]{1,2,0:T(8,128)}, ...), condition=%wide.region_22.23_spmd.clone.clone, body=%wide.region_16.22_spmd.clone.clone.sunk | while | flops 956698624 | bytes 86071088 | solution.py:333
  464.8 54.6 %while.126 = (s32[]{:T(128)}, f32[4,512]{1,0:T(4,128)S(1)}, bf16[4,512,4,64]{1,0,3,2:T(4,128)(2,1)S(1)}, s32[4]{0:T(128)S(1)}, s32[]{:T(128)}, /*index=5*/bf16[4...) while((s32[]{:T(128)}, f32[4,512]{1,0:T(4,128)S(1)}, ...), condition=%wide.region_19.19_spmd.clone, body=%wide.region_17.18_spmd.clone.sunk | while | flops 412093440 | bytes 32032952 | solution.py:281
  473.9 4.6 dynamic_update_slice.62
  487.6 4.6 dynamic_update_slice.62
  501.2 4.6 dynamic_update_slice.62
  514.9 4.6 dynamic_update_slice.62
  520.5 35.3 %while.127 = (s32[]{:T(128)}, f32[512,4,64]{0,2,1:T(8,128)}, f32[4,512,4,64]{1,3,2,0:T(8,128)}, bf16[4,512,4,64]{1,3,2,0:T(8,128)(2,1)S(1)}, s32[4]{0:T(128)S(1)...) while((s32[]{:T(128)}, f32[512,4,64]{0,2,1:T(8,128)}, ...), condition=%wide.region_21.21_spmd.clone, body=%wide.region_20.20_spmd.clone.sunk | while | flops 543425536 | bytes 17844388 | solution.py:315
  572.6 54.6 %while.126 = (s32[]{:T(128)}, f32[4,512]{1,0:T(4,128)S(1)}, bf16[4,512,4,64]{1,0,3,2:T(4,128)(2,1)S(1)}, s32[4]{0:T(128)S(1)}, s32[]{:T(128)}, /*index=5*/bf16[4...) while((s32[]{:T(128)}, f32[4,512]{1,0:T(4,128)S(1)}, ...), condition=%wide.region_19.19_spmd.clone, body=%wide.region_17.18_spmd.clone.sunk | while | flops 412093440 | bytes 32032952 | solution.py:281
  581.6 4.6 dynamic_update_slice.62
  595.3 4.6 dynamic_update_slice.62
  608.9 4.6 dynamic_update_slice.62
  622.6 4.6 dynamic_update_slice.62
  628.2 35.3 %while.127 = (s32[]{:T(128)}, f32[512,4,64]{0,2,1:T(8,128)}, f32[4,512,4,64]{1,3,2,0:T(8,128)}, bf16[4,512,4,64]{1,3,2,0:T(8,128)(2,1)S(1)}, s32[4]{0:T(128)S(1)...) while((s32[]{:T(128)}, f32[512,4,64]{0,2,1:T(8,128)}, ...), condition=%wide.region_21.21_spmd.clone, body=%wide.region_20.20_spmd.clone.sunk | while | flops 543425536 | bytes 17844388 | solution.py:315
  676.2 36.2 %reduce-scatter.10.cloned.1.call-done = bf16[2,512,256]{1,2,0:T(8,128)(2,1)} async-done(((bf16[2,2048,256]{1,2,0:T(8,128)(2,1)}), bf16[2,512,256]{1,2,0:T(8,128)(2,1)}) %reduce-scatter.10.cloned.1.call-update) | async-done | bytes 524304 | tf_op jit(solution)/shard_map/reduce_scatter | solution.py:337
  715.1 42.4 %reduce-scatter.12.cloned.1.call-done = bf16[2,512,256]{1,2,0:T(8,128)(2,1)} async-done(((bf16[2,2048,256]{1,2,0:T(8,128)(2,1)}), bf16[2,512,256]{1,2,0:T(8,128)(2,1)}) %reduce-scatter.12.cloned.1.call-update) | async-done | bytes 524304 | tf_op jit(solution)/shard_map/reduce_scatter | solution.py:340
  760.3 22.6 %all_to_all.64 = bf16[2,512,3,1,256]{4,0,3,2,1:T(2,128)(2,1)S(1)} all-to-all(bf16[2,512,3,1,256]{4,0,3,2,1:T(2,128)(2,1)S(1)} %copy.147), channel_id=1, replica_groups=mesh['slot'=2,'ctx'=4,'fsdp'=4] {'fsdp'}, dimensions={1} | all-to-all | bytes 3145728 | tf_op jit(solution)/shard_map/all_to_all | solution.py:356
  788.4 7.8 convolution_bitcast_fusion.2
  796.2 12.7 copy.150
  810.2 9.9 fusion.66
  821.1 9.7 fusion.76
  834.9 136.3 %reduce-scatter.22.cloned.1.call-done = f32[64,3072]{1,0:T(8,128)} async-done(((f32[1024,3072]{1,0:T(8,128)}), f32[64,3072]{1,0:T(8,128)}) %reduce-scatter.22.cloned.1.call-update) | async-done | bytes 786448
  973.6 178.4 %reduce-scatter.16.cloned.1.call-done = f32[64,4096]{1,0:T(8,128)} async-done(((f32[1024,4096]{1,0:T(8,128)}), f32[64,4096]{1,0:T(8,128)}) %reduce-scatter.16.cloned.1.call-update) | async-done | bytes 1048592 | tf_op jit(solution)/shard_map/reduce_scatter | solution.py:372
  1154.1 178.4 %reduce-scatter.18.cloned.1.call-done = f32[256,1024]{1,0:T(8,128)} async-done(((f32[4096,1024]{1,0:T(8,128)}), f32[256,1024]{1,0:T(8,128)}) %reduce-scatter.18.cloned.1.call-update) | async-done | bytes 1048592 | tf_op jit(solution)/shard_map/reduce_scatter | solution.py:374
  1338.5 53.4 %reduce-scatter.20.cloned.1.call-done = f32[64,128]{1,0:T(8,128)} async-done(((f32[1024,128]{1,0:T(8,128)}), f32[64,128]{1,0:T(8,128)}) %reduce-scatter.20.cloned.1.call-update) | async-done | bytes 32784 | tf_op jit(solution)/shard_map/reduce_scatter | solution.py:378
  1393.9 57.8 %all-reduce.15 = (bf16[3072]{0:T(1024)(128)(2,1)S(1)}, bf16[1024]{0:T(1024)(128)(2,1)S(1)}, bf16[1024]{0:T(1024)(128)(2,1)S(1)}, bf16[1024]{0:T(1024)(128)(2,1)S...) all-reduce(f32[3072]{0:T(1024)S(1)} %bitcast.284, ...), channel_id=7, replica_groups=mesh['slot'=2,'ctx'=4,'fsdp'=4] {'ctx','fsdp'}, use_global_device_ids=true, to_apply=%region_28.29.clone | all-reduce | flops 13312 | bytes 79872
  1452.3 8.2 all-reduce.17
  1465.4 5.7 fusion.60
  (525 shorter events, 384.1 us)
Async XLA Ops:
  7.2 74.6 %all-gather.10.cloned.1.call-start = ((), (), s32[]{:S(2)}) async-start(), calls=%async_computation.11 | async-start | bytes 6684672 | tf_op jit(solution)/shard_map/all_gather | solution.py:88
  7.9 160.0 %all-gather.18.cloned.1.call-start = ((), (), s32[]{:S(2)}) async-start(), calls=%async_computation.21 | async-start | bytes 2621440 | tf_op jit(solution)/shard_map/all_gather | solution.py:115
  124.8 89.7 %all-gather.20.cloned.1.call-start = ((), (), s32[]{:S(2)}) async-start(), calls=%async_computation.22 | async-start | bytes 2621440 | tf_op jit(solution)/shard_map/all_gather | solution.py:116
  125.6 267.5 %all-gather.12.cloned.1.call-start = ((), (), s32[]{:S(2)}) async-start(), calls=%async_computation.12 | async-start | bytes 2228224 | tf_op jit(solution)/shard_map/all_gather | solution.py:90
  126.1 270.1 %all-gather.14.cloned.1.call-start = ((), (), s32[]{:S(2)}) async-start(), calls=%async_computation.13 | async-start | bytes 8912896 | tf_op jit(solution)/shard_map/all_gather | solution.py:183
  126.7 286.0 %all-gather.16.cloned.1.call-start = ((), (), s32[]{:S(2)}) async-start(), calls=%async_computation.14 | async-start | bytes 8912896 | tf_op jit(solution)/shard_map/all_gather | solution.py:185
  167.9 50.6 %copy-start.48 = (s32[2]{0:T(128)S(1)}, s32[2]{0:T(128)}, u32[]{:S(2)}) copy-start(s32[2]{0:T(128)} %param.30) | copy-start | bytes 28
  218.5 132.9 %copy-start.47 = (bf16[256]{0:T(256)(128)(2,1)S(1)}, bf16[256]{0:T(256)(128)(2,1)}, u32[]{:S(2)}) copy-start(bf16[256]{0:T(256)(128)(2,1)} %param.38) | copy-start | bytes 1540
  218.5 153.0 %copy-start.34 = (bf16[64,128]{1,0:T(8,128)(2,1)S(1)}, bf16[64,128]{1,0:T(8,128)(2,1)}, u32[]{:S(2)}) copy-start(bf16[64,128]{1,0:T(8,128)(2,1)} %param.43) | copy-start | bytes 49156
  218.5 173.8 %copy-start.27 = (bf16[2,128,128]{2,1,0:T(8,128)(2,1)S(1)}, bf16[2,128,128]{2,1,0:T(8,128)(2,1)}, u32[]{:S(2)}) copy-start(bf16[2,128,128]{2,1,0:T(8,128)(2,1)} %param.45) | copy-start | bytes 196612
  255.9 19.2 %copy-start.18 = (bf16[2,512,256]{2,0,1:T(2,128)(2,1)S(1)}, bf16[2,512,256]{2,0,1:T(2,128)(2,1)}, u32[]{:S(2)}) copy-start(bf16[2,512,256]{2,0,1:T(2,128)(2,1)} %get-tuple-element.1734) | copy-start | bytes 1572868 | tf_op jit(solution)/shard_map/while
  320.9 19.2 %copy-start.18 = (bf16[2,512,256]{2,0,1:T(2,128)(2,1)S(1)}, bf16[2,512,256]{2,0,1:T(2,128)(2,1)}, u32[]{:S(2)}) copy-start(bf16[2,512,256]{2,0,1:T(2,128)(2,1)} %get-tuple-element.1734) | copy-start | bytes 1572868 | tf_op jit(solution)/shard_map/while
  347.8 44.6 %all-to-all-start.1 = ((bf16[2,512,1,256]{3,0,2,1:T(2,128)(2,1)}), bf16[2,512,1,256]{3,0,2,1:T(2,128)(2,1)S(1)}, u32[]{:S(2)}, u32[]{:S(2)}) async-start(bf16[2,512,1,256]{3,0,2,1:T(2,128)(2,1)} %bitcast.280), calls=%async_computation.1 | async-start | bytes 1048576 | tf_op jit(solution)/shard_map/all_to_all | solution.py:165
  351.4 86.2 %copy-start.22 = (f32[1024]{0:T(1024)}, f32[1024]{0:T(1024)S(1)}, u32[]{:S(2)}) copy-start(f32[1024]{0:T(1024)S(1)} %convert_element_type.200) | copy-start | bytes 12292
  351.4 61.3 %copy-start.24 = (f32[1024]{0:T(1024)}, f32[1024]{0:T(1024)S(1)}, u32[]{:S(2)}) copy-start(f32[1024]{0:T(1024)S(1)} %convert_element_type.201) | copy-start | bytes 12292
  392.3 27.2 %copy-start.16 = (bf16[1024,128]{1,0:T(8,128)(2,1)}, bf16[1024,128]{1,0:T(8,128)(2,1)S(1)}, u32[]{:S(2)}) copy-start(bf16[1024,128]{1,0:T(8,128)(2,1)S(1)} %all_gather.64) | copy-start | bytes 786436
  392.4 27.1 %copy-start.20 = (bf16[256,128]{1,0:T(8,128)(2,1)}, bf16[256,128]{1,0:T(8,128)(2,1)S(1)}, u32[]{:S(2)}) copy-start(bf16[256,128]{1,0:T(8,128)(2,1)S(1)} %bitcast_select_fusion) | copy-start | bytes 196612
  393.0 19.7 %copy-start.9 = (bf16[32,8,4,256]{3,1,2,0:T(8,128)(2,1)}, bf16[32,8,4,256]{3,1,2,0:T(8,128)(2,1)S(1)}, u32[]{:S(2)}) copy-start(bf16[32,8,4,256]{3,1,2,0:T(8,128)(2,1)S(1)} %copy.173) | copy-start | bytes 1572868
  395.9 41.7 %copy-start.3 = (f32[256,1024]{1,0:T(8,128)}, f32[256,1024]{1,0:T(8,128)S(1)}, u32[]{:S(2)}) copy-start(f32[256,1024]{1,0:T(8,128)S(1)} %get-tuple-element.1152) | copy-start | bytes 3145732
  395.9 41.7 %copy-start.28 = (f32[256]{0:T(256)}, f32[256]{0:T(256)S(1)}, u32[]{:S(2)}) copy-start(f32[256]{0:T(256)S(1)} %broadcast_multiply_fusion.3) | copy-start | bytes 3076
  396.2 41.4 %copy-start.30 = (f32[256]{0:T(256)}, f32[256]{0:T(256)S(1)}, u32[]{:S(2)}) copy-start(f32[256]{0:T(256)S(1)} %fusion.63) | copy-start | bytes 3076
  412.7 6.8 copy-start.46
  419.6 3.6 copy-start.44
  422.8 7.2 copy-start.11
  430.1 7.5 copy-start.15
  442.5 12.3 all-to-all-start.2
  446.0 266.3 %reduce-scatter.10.cloned.1.call-start = ((), (), s32[]{:S(2)}) async-start(), calls=%async_computation.15 | async-start | bytes 2621440 | tf_op jit(solution)/shard_map/reduce_scatter | solution.py:337
  558.5 4.1 copy-start.1
  666.2 4.2 copy-start.1
  671.3 86.2 %reduce-scatter.12.cloned.1.call-start = ((), (), s32[]{:S(2)}) async-start(), calls=%async_computation.16 | async-start | bytes 2621440 | tf_op jit(solution)/shard_map/reduce_scatter | solution.py:340
  672.1 161.3 %reduce-scatter.14.cloned.1.call-start = ((), (), s32[]{:S(2)}) async-start(), calls=%async_computation.17 | async-start | bytes 4456448 | tf_op jit(solution)/shard_map/reduce_scatter | solution.py:368
  675.2 296.0 %reduce-scatter.22.cloned.1.call-start = ((), (), s32[]{:S(2)}) async-start(), calls=%async_computation.23 | async-start | bytes 13369344
  788.4 7.8 copy-start.5
  809.0 343.0 %reduce-scatter.16.cloned.1.call-start = ((), (), s32[]{:S(2)}) async-start(), calls=%async_computation.18 | async-start | bytes 17825792 | tf_op jit(solution)/shard_map/reduce_scatter | solution.py:372
  820.0 512.4 %reduce-scatter.18.cloned.1.call-start = ((), (), s32[]{:S(2)}) async-start(), calls=%async_computation.19 | async-start | bytes 17825792 | tf_op jit(solution)/shard_map/reduce_scatter | solution.py:374
  830.8 561.2 %reduce-scatter.20.cloned.1.call-start = ((), (), s32[]{:S(2)}) async-start(), calls=%async_computation.20 | async-start | bytes 557056 | tf_op jit(solution)/shard_map/reduce_scatter | solution.py:378
  831.8 504.7 %copy-start.17 = (bf16[1024,128]{1,0:T(8,128)(2,1)S(1)}, bf16[1024,128]{1,0:T(8,128)(2,1)}, u32[]{:S(2)}) copy-start(bf16[1024,128]{1,0:T(8,128)(2,1)} %copy-done.16) | copy-start | bytes 786436
  833.0 638.1 %all-reduce.21.cloned.1.call-start = ((), (), s32[]{:S(2)}) async-start(), calls=%async_computation.24 | async-start | bytes 3932160 | tf_op jit(solution)/shard_map/psum | solution.py:381
  973.5 420.3 %copy-start.32 = (f32[1024]{0:T(1024)S(1)}, f32[1024]{0:T(1024)}, u32[]{:S(2)}) copy-start(f32[1024]{0:T(1024)} %get-tuple-element.1109) | copy-start | bytes 12292
  973.5 420.3 %copy-start.33 = (f32[1024]{0:T(1024)S(1)}, f32[1024]{0:T(1024)}, u32[]{:S(2)}) copy-start(f32[1024]{0:T(1024)} %get-tuple-element.1113) | copy-start | bytes 12292
  973.5 420.3 %copy-start.35 = (f32[4096]{0:T(1024)S(1)}, f32[4096]{0:T(1024)}, u32[]{:S(2)}) copy-start(f32[4096]{0:T(1024)} %get-tuple-element.1111) | copy-start | bytes 49156
  973.5 420.4 %copy-start.36 = (f32[1024]{0:T(1024)S(1)}, f32[1024]{0:T(1024)}, u32[]{:S(2)}) copy-start(f32[1024]{0:T(1024)} %get-tuple-element.967) | copy-start | bytes 12292
  973.5 420.4 %copy-start.37 = (f32[1024]{0:T(1024)S(1)}, f32[1024]{0:T(1024)}, u32[]{:S(2)}) copy-start(f32[1024]{0:T(1024)} %get-tuple-element.971) | copy-start | bytes 12292
  973.5 420.4 %copy-start.38 = (f32[1024]{0:T(1024)S(1)}, f32[1024]{0:T(1024)}, u32[]{:S(2)}) copy-start(f32[1024]{0:T(1024)} %get-tuple-element.969) | copy-start | bytes 12292
  973.5 420.4 %copy-start.39 = (f32[1024]{0:T(1024)S(1)}, f32[1024]{0:T(1024)}, u32[]{:S(2)}) copy-start(f32[1024]{0:T(1024)} %get-tuple-element.972) | copy-start | bytes 12292
  973.5 491.9 %copy-start.6 = (bf16[256,3072]{1,0:T(8,128)(2,1)S(1)}, bf16[256,3072]{1,0:T(8,128)(2,1)}, u32[]{:S(2)}) copy-start(bf16[256,3072]{1,0:T(8,128)(2,1)} %copy-done.5) | copy-start | bytes 4718596
  973.6 491.9 %copy-start.41 = (f32[256]{0:T(256)S(1)}, f32[256]{0:T(256)}, u32[]{:S(2)}) copy-start(f32[256]{0:T(256)} %copy-done.40) | copy-start | bytes 3076
  1471.1 6.5 copy-start.26
  (28 other events, 38.6 us)
Sparse Core Ops, SparseCore 0:
  10.3 64.6 all-gather.9
  124.9 42.8 all-gather.17
  170.0 44.4 all-gather.19
  216.5 40.3 all-gather.11
  258.9 73.0 all-gather.13
  334.0 75.3 all-gather.15
  671.4 40.8 reduce-scatter.9
  714.6 42.8 reduce-scatter.11
  761.4 71.9 reduce-scatter.13
  837.2 133.9 reduce-scatter.21
  975.3 176.6 reduce-scatter.15
  1156.0 176.4 reduce-scatter.17
  1336.6 55.3 reduce-scatter.19
  1395.4 59.3 all-reduce.20
where the time goes:
time: 1500 us; the launch traced here: 1490 us
  waiting for transfers between devices  720 us (48%)
  matrix products  237 us (16%)
  blocking collectives  217 us (14%)
  local copies, waits for them, and re-layouts  179 us (12%)
  other arithmetic  103 us (7%)
  between operations  18.4 us (1%)
    reduce_scatter x1, waiting for transfers between devices, per_device(): lax.psum_scatter(d_up, ('ctx', 'fsdp'), scatter_dimension=0, tiled=True)  178 us
    reduce_scatter x1, waiting for transfers between devices, per_device(): lax.psum_scatter(d_down, ('ctx', 'fsdp'), scatter_dimension=0, tiled=True)  178 us
    unnamed x15, waiting for transfers between devices  140 us
    unnamed x2, blocking collectives  123 us
    reduce_scatter x1, waiting for transfers between devices, per_device(): lax.psum_scatter(d_proj, ('ctx', 'fsdp'), scatter_dimension=0, tiled=True)  53.4 us
    lt x32, other arithmetic, block_scores(): return jnp.where((key_ids < length)[None, None, :], scores, NEG_FILL)  45.4 us
    all_gather x1, waiting for transfers between devices, per_device(): lax.all_gather(local_values, 'ctx', axis=1, tiled=True)  42.7 us
    reduce_scatter x1, waiting for transfers between devices, per_device(): lax.psum_scatter(value_terms.astype(jnp.bfloat16), 'ctx', scatter_dimensi...  42.4 us
  transfers between devices with their start and end apart: 16, of which 9 were waited for; matrix products, arithmetic and copies ran while one was open for 16% of the time, Pallas kernels for 0%

commit v1 on v0

--- a/solution.py
+++ b/solution.py
@@ -3,14 +3,562 @@
 import jax
 import jax.numpy as jnp
 from jax import lax
+from jax.experimental import pallas as pl
+from jax.experimental.pallas import tpu as pltpu
+from jax.sharding import Mesh
 from jax.sharding import PartitionSpec as P
 
 H = 16
 HD = 64
-
-
+LN_EPS = 1e-05
 NEG_FILL = -1e30
-LN_EPS = 1e-05
+F32 = jnp.float32
+BF16 = jnp.bfloat16
+GROUP = ("ctx", "x", "core")
+LANE = ("ctx", "x")
+SWAP = [(0, 1), (1, 0)]
+VMEM_LIMIT = 60 * 1024 * 1024
+
+
+def mm(left, right):
+    return jnp.dot(left, right, preferred_element_type=F32)
+
+
+def contract(left, right, left_dim, right_dim):
+    return lax.dot_general(
+        left, right, (((left_dim,), (right_dim,)), ((), ())), preferred_element_type=F32
+    )
+
+
+def swap_core(value):
+    return lax.ppermute(value, "core", SWAP)
+
+
+def swap_slot(value):
+    return lax.ppermute(value, "slot", SWAP)
+
+
+def pick(stacked, index, axis):
+    return lax.dynamic_index_in_dim(stacked, index, axis, keepdims=False)
+
+
+def project_kernel(tok_ref, w_ref, b_ref, cos_ref, sin_ref, q_ref, k_ref, v_ref):
+    joined = mm(tok_ref[...], w_ref[...]) + b_ref[...]
+    wide = 2 * HD
+    turned = joined[:, :wide] * cos_ref[...] + joined[:, wide : 2 * wide] * sin_ref[...]
+    q_ref[...] = (turned[:, :HD].astype(BF16) * HD ** (-0.5)).astype(BF16)
+    k_ref[...] = turned[:, HD:].astype(BF16)
+    v_ref[...] = joined[:, 2 * wide :].astype(BF16)
+
+
+def project(tokens, weight, bias, cosine, sine):
+    rows, width = tokens.shape
+    seq = cosine.shape[0]
+    block = min(512, seq)
+    per_slot = seq // block
+    cols = weight.shape[1]
+    head_out = jax.ShapeDtypeStruct((rows, HD), BF16)
+    head_spec = pl.BlockSpec((block, HD), lambda i: (i, 0))
+    return pl.pallas_call(
+        project_kernel,
+        grid=(rows // block,),
+        in_specs=[
+            pl.BlockSpec((block, width), lambda i: (i, 0)),
+            pl.BlockSpec((width, cols), lambda i: (0, 0)),
+            pl.BlockSpec((1, cols), lambda i: (0, 0)),
+            pl.BlockSpec((block, 2 * HD), lambda i: (i % per_slot, 0)),
+            pl.BlockSpec((block, 2 * HD), lambda i: (i % per_slot, 0)),
+        ],
+        out_specs=[head_spec] * 3,
+        out_shape=[head_out] * 3,
+        compiler_params=pltpu.CompilerParams(vmem_limit_bytes=VMEM_LIMIT),
+        cost_estimate=pl.CostEstimate(
+            flops=2 * rows * width * cols, bytes_accessed=2 * rows * width, transcendentals=0
+        ),
+        name="project",
+    )(tokens, weight, bias, cosine, sine)
+
+
+QB = 512
+KB = 512
+
+
+def forward_kernel(
+    len_ref, core_ref, q_ref, k_ref, v_ref, out_ref, send_ref, norm_ref, *, part
+):
+    length = len_ref[pl.program_id(0)]
+    core = core_ref[0]
+    queries = q_ref[0]
+    rows = queries.shape[0]
+
+    def step(j, state):
+        highest, total, mix = state
+        start = pl.multiple_of(j * KB, KB)
+        scores = contract(queries, k_ref[0, pl.ds(start, KB), :], 1, 1)
+        ids = start + lax.broadcasted_iota(jnp.int32, (1, KB), 1)
+        scores = jnp.where(ids < length, scores, NEG_FILL)
+        higher = jnp.maximum(highest, jnp.max(scores, axis=1, keepdims=True))
+        fade = jnp.exp(highest - higher)
+        weights = jnp.exp(scores - higher)
+        total = total * fade + jnp.sum(weights, axis=1, keepdims=True)
+        mix = mix * fade + mm(weights.astype(BF16), v_ref[0, pl.ds(start, KB), :])
+        return higher, total, mix
+
+    blocks = (length + KB - 1) // KB
+    highest, total, mix = lax.fori_loop(
+        0,
+        blocks,
+        step,
+        (
+            jnp.full((rows, 1), NEG_FILL, F32),
+            jnp.zeros((rows, 1), F32),
+            jnp.zeros((rows, HD), F32),
+        ),
+    )
+    mix = mix / total
+    out_ref[0] = mix
+    log_norm = jnp.broadcast_to(highest + jnp.log(total), (rows, 128))
+    norm_ref[0] = jnp.transpose(log_norm)[0:1, :]
+    low = mix.astype(BF16)
+    for chip in range(rows // (2 * part)):
+        for half in range(2):
+            at = (2 * chip + half) * part
+            send_ref[chip, half ^ core, 0] = low[at : at + part]
+
+
+def attend(lengths, core, queries, keys, values, part):
+    slots, seq, _ = queries.shape
+    chips = seq // (2 * part)
+    spec_q = pl.BlockSpec((1, QB, HD), lambda s, i, *_: (s, i, 0))
+    spec_k = pl.BlockSpec((1, seq, HD), lambda s, i, *_: (s, 0, 0))
+    return pl.pallas_call(
+        partial(forward_kernel, part=part),
+        grid_spec=pltpu.PrefetchScalarGridSpec(
+            num_scalar_prefetch=2,
+            grid=(slots, seq // QB),
+            in_specs=[spec_q, spec_k, spec_k],
+            out_specs=[
+                spec_q,
+                pl.BlockSpec(
+                    (QB // (2 * part), 2, 1, part, HD), lambda s, i, *_: (i, 0, s, 0, 0)
+                ),
+                pl.BlockSpec((1, 1, QB), lambda s, i, *_: (s, 0, i)),
+            ],
+        ),
+        out_shape=[
+            jax.ShapeDtypeStruct((slots, seq, HD), F32),
+            jax.ShapeDtypeStruct((chips, 2, slots, part, HD), BF16),
+            jax.ShapeDtypeStruct((slots, 1, seq), F32),
+        ],
+        compiler_params=pltpu.CompilerParams(vmem_limit_bytes=VMEM_LIMIT),
+        cost_estimate=pl.CostEstimate(
+            flops=16 * slots * seq * seq * HD,
+            bytes_accessed=8 * slots * seq * HD,
+            transcendentals=slots * seq * seq,
+        ),
+        name="attend",
+    )(lengths, core, queries, keys, values)
+
+
+def backward_kernel(
+    len_ref, q_ref, k_ref, v_ref, g_ref, norm_ref, dot_ref, dq_ref, dk_ref, dv_ref, dqt
+):
+    length = len_ref[pl.program_id(0)]
+    j = pl.program_id(1)
+    start = j * KB
+    key_block = k_ref[0]
+    value_block = v_ref[0]
+
+    @pl.when(j == 0)
+    def _():
+        dqt[...] = jnp.zeros_like(dqt)
+
+    turned = jnp.transpose(key_block.astype(F32)).astype(BF16)
+    ids = start + lax.broadcasted_iota(jnp.int32, (KB, 1), 0)
+    shift = jnp.where(ids < length, 0.0, NEG_FILL)
+
+    def step(i, state):
+        key_grad, value_grad = state
+        at = pl.multiple_of(i * QB, QB)
+        queries = q_ref[0, pl.ds(at, QB), :]
+        grads = g_ref[0, pl.ds(at, QB), :]
+        scores = contract(key_block, queries, 1, 1) + shift
+        probs = jnp.exp(scores - norm_ref[0, :, pl.ds(at, QB)])
+        grad_probs = contract(value_block, grads, 1, 1)
+        grad_scores = (probs * (grad_probs - dot_ref[0, :, pl.ds(at, QB)])).astype(BF16)
+        value_grad = value_grad + mm(probs.astype(BF16), grads)
+        key_grad = key_grad + mm(grad_scores, queries)
+        dqt[:, pl.ds(at, QB)] += mm(turned, grad_scores)
+        return key_grad, value_grad
+
+    blocks = jnp.where(start < length, (length + QB - 1) // QB, 0)
+    zero = jnp.zeros((KB, HD), F32)
+    key_grad, value_grad = lax.fori_loop(0, blocks, step, (zero, zero))
+    dk_ref[0] = key_grad
+    dv_ref[0] = value_grad
+
+    @pl.when(j == pl.num_programs(1) - 1)
+    def _():
+        dq_ref[0] = jnp.transpose(dqt[...])
+
+
+def attend_back(lengths, queries, keys, values, grads, norms, dots):
+    slots, seq, _ = queries.shape
+    whole = pl.BlockSpec((1, seq, HD), lambda s, j, *_: (s, 0, 0))
+    block = pl.BlockSpec((1, KB, HD), lambda s, j, *_: (s, j, 0))
+    row = pl.BlockSpec((1, 1, seq), lambda s, j, *_: (s, 0, 0))
+    out = jax.ShapeDtypeStruct((slots, seq, HD), F32)
+    return pl.pallas_call(
+        backward_kernel,
+        grid_spec=pltpu.PrefetchScalarGridSpec(
+            num_scalar_prefetch=1,
+            grid=(slots, seq // KB),
+            in_specs=[whole, block, block, whole, row, row],
+            out_specs=[whole, block, block],
+            scratch_shapes=[pltpu.VMEM((HD, seq), F32)],
+        ),
+        out_shape=[out] * 3,
+        compiler_params=pltpu.CompilerParams(vmem_limit_bytes=VMEM_LIMIT),
+        cost_estimate=pl.CostEstimate(
+            flops=40 * slots * seq * seq * HD,
+            bytes_accessed=20 * slots * seq * HD,
+            transcendentals=slots * seq * seq,
+        ),
+        name="attend_back",
+    )(lengths, queries, keys, values, grads, norms, dots)
+
+
+def norm_forward(values, gain, shift):
+    center = values - jnp.mean(values, axis=-1, keepdims=True)
+    spread = jnp.mean(center * center, axis=-1, keepdims=True)
+    root = lax.rsqrt(spread + LN_EPS)
+    unit = center * root
+    return unit * gain + shift, unit, root
+
+
+def norm_backward(grad, unit, root, gain):
+    scaled = grad * gain
+    inner = scaled - jnp.mean(scaled, axis=-1, keepdims=True)
+    inner = inner - unit * jnp.mean(scaled * unit, axis=-1, keepdims=True)
+    return root * inner, jnp.sum(grad * unit, axis=0), jnp.sum(grad, axis=0)
+
+
+def gelu_pair(values):
+    half = 0.5 + 0.5 * lax.erf(values * 0.7071067811865476)
+    bell = jnp.exp(-0.5 * values * values) * 0.3989422804014327
+    return values * half, half + values * bell
+
+
+def rope_rows(positions):
+    halfway = HD // 2
+    ladder = jnp.arange(halfway, dtype=F32) * (2.0 / HD)
+    frequency = jnp.power(jnp.float32(10000.0), -ladder)
+    angles = positions[:, None] * frequency[None, :]
+    return jnp.cos(angles), jnp.sin(angles)
+
+
+def head_device(
+    tokens,
+    lengths,
+    w_qkv,
+    b_qkv,
+    w_out,
+    b_out,
+    ln1_gain,
+    ln1_bias,
+    w_up,
+    b_up,
+    w_down,
+    b_down,
+    ln2_gain,
+    ln2_bias,
+    w_proj,
+    cot_out,
+    cot_emb,
+):
+    n_lane = lax.axis_size("ctx") * lax.axis_size("x")
+    n_group = 2 * n_lane
+    core = lax.axis_index("core")
+    slot = lax.axis_index("slot")
+    chip = lax.axis_index("ctx") * lax.axis_size("x") + lax.axis_index("x")
+    me = 2 * chip + core
+    slots, part, width = tokens.shape
+    seq = part * n_group
+    rows = slots * part
+    shard = width // n_group
+    ff_shard = w_down.shape[0]
+    ff_half = ff_shard // 2
+    proj = w_proj.shape[1]
+    head_cols = 3 * HD
+
+    small = jnp.concatenate(
+        [b_qkv, b_out, ln1_gain, ln1_bias, b_up, b_down, ln2_gain, ln2_bias]
+    )
+    small_at = [0]
+    for piece in (b_qkv, b_out, ln1_gain, ln1_bias, b_up, b_down, ln2_gain, ln2_bias):
+        small_at.append(small_at[-1] + piece.shape[0])
+    small_rows = -(-small.shape[0] // proj)
+    small_rows = -(-small_rows // 16) * 16
+    small = jnp.pad(small, (0, small_rows * proj - small.shape[0])).reshape(small_rows, proj)
+    packed = lax.all_gather(jnp.concatenate([w_proj, small], axis=0), GROUP, axis=0, tiled=False)
+    proj_full = packed[:, :shard].reshape(width, proj)
+    smalls = packed[:, shard:].reshape(n_group, small_rows * proj).astype(F32)
+    qkv_bias, out_bias, gain_one, shift_one, up_bias, down_bias, gain_two, shift_two = (
+        smalls[:, a:b].reshape(-1) for a, b in zip(small_at[:-1], small_at[1:])
+    )
+
+    by_head = w_qkv.reshape(shard, 3, n_group, HD).transpose(2, 0, 1, 3)
+    my_head = lax.all_to_all(by_head.reshape(n_group, shard, head_cols), GROUP, 0, 0, tiled=True)
+    my_head = my_head.reshape(width, 3, HD)
+    all_tokens = lax.all_gather(tokens, GROUP, axis=1, tiled=True).reshape(slots * seq, width)
+
+    def with_swapped(joined):
+        first = joined[:, 0:2]
+        halves = first.reshape(-1, 2, 2, HD // 2)
+        swapped = jnp.stack([-halves[:, :, 1], halves[:, :, 0]], axis=2)
+        return jnp.concatenate(
+            [
+                first.reshape(-1, 2 * HD),
+                swapped.reshape(-1, 2 * HD),
+                joined[:, 2],
+            ],
+            axis=1,
+        )
+
+    head_weight = with_swapped(my_head)
+    head_bias = with_swapped(pick(qkv_bias.reshape(1, 3, n_group, HD), me, 2))
+    cosine, sine = rope_rows(jnp.arange(seq, dtype=jnp.int32).astype(F32))
+    cos_wide = jnp.tile(cosine, (1, 4))
+    sin_wide = jnp.tile(sine, (1, 4))
+    queries, keys, values = project(all_tokens, head_weight, head_bias, cos_wide, sin_wide)
+    queries, keys, values = (t.reshape(slots, seq, HD) for t in (queries, keys, values))
+
+    def two_lanes(mine, theirs):
+        low_first = jnp.stack([mine, theirs], axis=0)
+        high_first = jnp.stack([theirs, mine], axis=0)
+        return jnp.where(core == 0, low_first, high_first)
+
+    out_lane = lax.all_gather(w_out, LANE, axis=0, tiled=True)
+    up_split = w_up.reshape(shard, n_lane, 2, 2, ff_half)
+    up_mine = pick(up_split, core, 2)
+    up_theirs = swap_core(pick(up_split, 1 - core, 2))
+    up_chip = two_lanes(up_mine, up_theirs).reshape(2 * shard, n_lane, 2, ff_half)
+    down_split = w_down.reshape(2, ff_half, width)
+    ups, downs = [], []
+    for half in (slot, 1 - slot):
+        up_part = pick(up_chip, half, 2).reshape(2 * shard, n_lane * ff_half)
+        ups.append(lax.all_gather(up_part, LANE, axis=0, tiled=True))
+        downs.append(lax.all_gather(pick(down_split, half, 0), LANE, axis=0, tiled=True))
+    bias_lane = pick(up_bias.reshape(n_lane, 2, 2, ff_half), core, 1)
+    up_biases = [pick(bias_lane, half, 1).reshape(-1) for half in (slot, 1 - slot)]
+
+    qkv_split = w_qkv.reshape(shard, 3, n_lane, 2, HD)
+    qkv_mine = pick(qkv_split, core, 3)
+    qkv_theirs = swap_core(pick(qkv_split, 1 - core, 3))
+    qkv_chip = two_lanes(qkv_mine, qkv_theirs).transpose(0, 1, 3, 2, 4)
+    qkv_lane = lax.all_gather(
+        qkv_chip.reshape(2 * shard, n_lane * head_cols), LANE, axis=0, tiled=True
+    )
+
+    mixture, send, norms = attend(
+        lengths, core.reshape(1).astype(jnp.int32), queries, keys, values, part
+    )
+    merged = lax.all_to_all(send, LANE, 0, 0, tiled=True)
+    merged = merged.transpose(1, 2, 3, 0, 4).reshape(2 * rows, n_lane * HD)
+
+    def own_sum(partial_rows):
+        return partial_rows[:rows] + swap_core(partial_rows[rows:])
+
+    def both(value):
+        return jnp.concatenate([value, swap_core(value)], axis=0)
+
+    flat_tokens = tokens.reshape(rows, width).astype(F32)
+    attended = own_sum(mm(merged, out_lane)) + out_bias
+    hidden_one, unit_one, root_one = norm_forward(flat_tokens + attended, gain_one, shift_one)
+    hidden_low = both(hidden_one.astype(BF16))
+
+    actives, slopes = [], []
+    downward = None
+    for up, bias, down in zip(ups, up_biases, downs):
+        active, slope = gelu_pair(mm(hidden_low, up) + bias)
+        active = active.astype(BF16)
+        actives.append(active)
+        slopes.append(slope)
+        term = mm(active, down)
+        downward = term if downward is None else downward + term
+    downward = own_sum(downward) + down_bias
+    out_rows, unit_two, root_two = norm_forward(hidden_one + downward, gain_two, shift_two)
+    out_low = out_rows.astype(BF16)
+    embeds = mm(out_low, proj_full).astype(BF16)
+
+    place = me * part + jnp.arange(part, dtype=jnp.int32)
+    live = (place[None, :] < lengths[:, None]).reshape(rows, 1)
+    grad_out = jnp.where(live, cot_out.reshape(rows, width).astype(F32), 0.0)
+    grad_emb = jnp.where(live, cot_emb.reshape(rows, proj), 0)
+    d_proj = contract(out_low, grad_emb, 0, 0)
+    grad_full = grad_out + contract(grad_emb, proj_full, 1, 1)
+    grad_two, d_gain_two, d_shift_two = norm_backward(grad_full, unit_two, root_two, gain_two)
+    grad_down_own = grad_two.astype(BF16)
+    d_down_bias = jnp.sum(grad_down_own.astype(F32), axis=0)
+    grad_down = both(grad_down_own)
+
+    d_ups, d_downs, d_up_biases = [], [], []
+    grad_hidden = None
+    for up, down, active, slope in zip(ups, downs, actives, slopes):
+        grad_up = (contract(grad_down, down, 1, 1) * slope).astype(BF16)
+        d_downs.append(contract(active, grad_down, 0, 0).astype(BF16))
+        d_ups.append(contract(hidden_low, grad_up, 0, 0).astype(BF16))
+        d_up_biases.append(jnp.sum(grad_up.astype(F32), axis=0))
+        term = contract(grad_up, up, 1, 1)
+        grad_hidden = term if grad_hidden is None else grad_hidden + term
+    grad_hidden = grad_two + own_sum(grad_hidden)
+    grad_one, d_gain_one, d_shift_one = norm_backward(grad_hidden, unit_one, root_one, gain_one)
+    grad_att_own = grad_one.astype(BF16)
+    d_out_bias = jnp.sum(grad_att_own.astype(F32), axis=0)
+    grad_att = both(grad_att_own)
+    grad_merged = contract(grad_att, out_lane, 1, 1).astype(BF16)
+    grad_merged = grad_merged.reshape(2, slots, part, n_lane, HD).transpose(3, 0, 1, 2, 4)
+    grad_heads = lax.all_to_all(grad_merged, LANE, 0, 0, tiled=True)
+
+    def core_order(value):
+        return jnp.where(core == 0, value, jnp.flip(value, axis=1))
+
+    grad_heads = core_order(grad_heads).transpose(2, 0, 1, 3, 4).reshape(slots, seq, HD)
+
+    half_width = width // 2
+    att_split = grad_att.reshape(2 * rows, 2, half_width)
+    d_outs = [
+        contract(merged, pick(att_split, half, 1), 0, 0).astype(BF16)
+        for half in (slot, 1 - slot)
+    ]
+
+    def reduced(pair):
+        both_slots = pair[0].astype(F32) + swap_slot(pair[1]).astype(F32)
+        return lax.psum_scatter(both_slots.astype(BF16), LANE, scatter_dimension=0, tiled=True)
+
+    red_down = reduced(d_downs)
+    red_up = reduced(d_ups)
+    red_out = reduced(d_outs)
+
+    def halves(mine, axis):
+        theirs = swap_slot(mine)
+        return jnp.where(
+            slot == 0, jnp.stack([mine, theirs], axis), jnp.stack([theirs, mine], axis)
+        )
+
+    grad_w_down = halves(red_down, 0).reshape(ff_shard, width).astype(F32)
+    grad_w_out = halves(red_out, 1).reshape(shard, width).astype(F32)
+    up_rows = red_up.reshape(2, shard, n_lane, ff_half)
+    up_keep = pick(up_rows, core, 0)
+    up_got = swap_core(pick(up_rows, 1 - core, 0))
+    up_lanes = jnp.where(
+        core == 0, jnp.stack([up_keep, up_got], 2), jnp.stack([up_got, up_keep], 2)
+    )
+    grad_w_up = halves(up_lanes, 3).reshape(shard, w_up.shape[1]).astype(F32)
+
+    up_bias_grad = jnp.stack(d_up_biases, axis=0)
+    up_bias_grad = jnp.where(slot == 0, up_bias_grad, jnp.flip(up_bias_grad, axis=0))
+    up_bias_grad = up_bias_grad.reshape(2, n_lane, ff_half).transpose(1, 0, 2)
+    zero_lane = jnp.zeros_like(up_bias_grad)
+    up_bias_grad = jnp.where(
+        core == 0,
+        jnp.stack([up_bias_grad, zero_lane], 1),
+        jnp.stack([zero_lane, up_bias_grad], 1),
+    )
+    vectors = (
+        d_out_bias,
+        d_gain_one,
+        d_shift_one,
+        up_bias_grad.reshape(-1),
+        d_down_bias,
+        d_gain_two,
+        d_shift_two,
+    )
+    small_grad = jnp.concatenate([v.reshape(n_group, -1) for v in vectors], axis=1)
+    small_cols = small_grad.shape[1]
+    vec_rows = -(-small_cols // proj)
+    vec_rows = -(-vec_rows // 8) * 8
+    small_grad = jnp.pad(small_grad, ((0, 0), (0, vec_rows * proj - small_cols)))
+    small_grad = jnp.concatenate(
+        [d_proj.reshape(n_group, shard, proj), small_grad.reshape(n_group, vec_rows, proj)], axis=1
+    )
+    small_red = lax.psum_scatter(
+        small_grad.reshape(n_group * (shard + vec_rows), proj), GROUP, scatter_dimension=0, tiled=True
+    )
+    small_low = small_red.astype(BF16)
+    small_sum = small_low.astype(F32) + swap_slot(small_low).astype(F32)
+    grad_w_proj = small_sum[:shard]
+    vec_sum = small_sum[shard:].reshape(-1)
+    vec_outs = []
+    at = 0
+    for v in vectors:
+        size = v.size // n_group
+        vec_outs.append(vec_sum[at : at + size])
+        at += size
+    (
+        grad_b_out,
+        grad_gain_one,
+        grad_shift_one,
+        grad_b_up,
+        grad_b_down,
+        grad_gain_two,
+        grad_shift_two,
+    ) = vec_outs
+
+    row_dots = jnp.sum(grad_heads.astype(F32) * mixture, axis=-1).reshape(slots, 1, seq)
+    grad_q, grad_k, grad_v = attend_back(
+        lengths, queries, keys, values, grad_heads, norms, row_dots
+    )
+
+    def turn_back(value):
+        first, second = value[..., : HD // 2], value[..., HD // 2 :]
+        return jnp.concatenate(
+            [first * cosine + second * sine, second * cosine - first * sine], axis=-1
+        )
+
+    grad_joined = jnp.concatenate(
+        [turn_back(grad_q * HD ** (-0.5)), turn_back(grad_k), grad_v], axis=-1
+    ).astype(BF16)
+    d_qkv = contract(all_tokens, grad_joined.reshape(slots * seq, head_cols), 0, 0)
+    d_qkv_bias = jnp.sum(grad_joined.astype(F32), axis=(0, 1))
+    d_qkv = jnp.concatenate(
+        [
+            d_qkv.reshape(n_group, shard, head_cols),
+            jnp.broadcast_to(d_qkv_bias, (n_group, 16, head_cols)),
+        ],
+        axis=1,
+    ).astype(BF16)
+    d_qkv = (d_qkv.astype(F32) + swap_slot(d_qkv).astype(F32)).astype(BF16)
+    d_qkv = lax.all_to_all(d_qkv, GROUP, 0, 0, tiled=True).astype(F32)
+    grad_w_qkv = (
+        d_qkv[:, :shard].reshape(n_group, shard, 3, HD).transpose(1, 2, 0, 3).reshape(shard, 3 * width)
+    )
+    qkv_bias_grad = d_qkv[:, shard].reshape(n_group, 3, HD).transpose(1, 0, 2).reshape(-1)
+    grad_b_qkv = lax.dynamic_slice(qkv_bias_grad, (me * b_qkv.shape[0],), (b_qkv.shape[0],))
+
+    to_chips = grad_joined.reshape(slots, n_lane, 2, part, head_cols).transpose(1, 2, 0, 3, 4)
+    joined_rows = lax.all_to_all(core_order(to_chips), LANE, 0, 0, tiled=True)
+    joined_rows = joined_rows.transpose(1, 2, 3, 0, 4).reshape(2 * rows, n_lane * head_cols)
+    input_grad = own_sum(contract(joined_rows, qkv_lane, 1, 1)) + grad_one
+
+    return (
+        out_low.reshape(slots, part, width),
+        embeds.reshape(slots, part, proj),
+        input_grad.astype(BF16).reshape(slots, part, width),
+        grad_w_qkv,
+        grad_b_qkv,
+        grad_w_out,
+        grad_b_out,
+        grad_gain_one,
+        grad_shift_one,
+        grad_w_up,
+        grad_b_up,
+        grad_w_down,
+        grad_b_down,
+        grad_gain_two,
+        grad_shift_two,
+        grad_w_proj,
+    )
 
 
 def layer_norm(hidden, gain, shift):
@@ -413,43 +961,52 @@
 
 
 def solution(mesh):
+    n_slot, n_ctx, n_fsdp = (mesh.shape[a] for a in ("slot", "ctx", "fsdp"))
+    rows_axes = ("ctx", "fsdp")
+    step = per_device
+    if n_slot == 2 and n_fsdp % 2 == 0 and n_ctx * n_fsdp == H:
+        mesh = Mesh(
+            mesh.devices.reshape(n_slot, n_ctx, n_fsdp // 2, 2), ("slot", "ctx", "x", "core")
+        )
+        rows_axes = GROUP
+        step = head_device
     in_specs = (
-        P("slot", ("ctx", "fsdp"), None),
+        P("slot", rows_axes, None),
         P("slot"),
-        P(("ctx", "fsdp"), None),
-        P(("ctx", "fsdp")),
-        P(("ctx", "fsdp"), None),
-        P(("ctx", "fsdp")),
-        P(("ctx", "fsdp")),
-        P(("ctx", "fsdp")),
-        P(("ctx", "fsdp"), None),
-        P(("ctx", "fsdp")),
-        P(("ctx", "fsdp"), None),
-        P(("ctx", "fsdp")),
-        P(("ctx", "fsdp")),
-        P(("ctx", "fsdp")),
-        P(("ctx", "fsdp"), None),
-        P("slot", ("ctx", "fsdp"), None),
-        P("slot", ("ctx", "fsdp"), None),
+        P(rows_axes, None),
+        P(rows_axes),
+        P(rows_axes, None),
+        P(rows_axes),
+        P(rows_axes),
+        P(rows_axes),
+        P(rows_axes, None),
+        P(rows_axes),
+        P(rows_axes, None),
+        P(rows_axes),
+        P(rows_axes),
+        P(rows_axes),
+        P(rows_axes, None),
+        P("slot", rows_axes, None),
+        P("slot", rows_axes, None),
     )
     out_specs = (
-        P("slot", ("ctx", "fsdp"), None),
-        P("slot", ("ctx", "fsdp"), None),
-        P("slot", ("ctx", "fsdp"), None),
-        P(("ctx", "fsdp"), None),
-        P(("ctx", "fsdp")),
-        P(("ctx", "fsdp"), None),
-        P(("ctx", "fsdp")),
-        P(("ctx", "fsdp")),
-        P(("ctx", "fsdp")),
-        P(("ctx", "fsdp"), None),
-        P(("ctx", "fsdp")),
-        P(("ctx", "fsdp"), None),
-        P(("ctx", "fsdp")),
-        P(("ctx", "fsdp")),
-        P(("ctx", "fsdp")),
-        P(("ctx", "fsdp"), None),
+        P("slot", rows_axes, None),
+        P("slot", rows_axes, None),
+        P("slot", rows_axes, None),
+        P(rows_axes, None),
+        P(rows_axes),
+        P(rows_axes, None),
+        P(rows_axes),
+        P(rows_axes),
+        P(rows_axes),
+        P(rows_axes, None),
+        P(rows_axes),
+        P(rows_axes, None),
+        P(rows_axes),
+        P(rows_axes),
+        P(rows_axes),
+        P(rows_axes, None),
     )
     return jax.shard_map(
-        per_device, mesh=mesh, in_specs=in_specs, out_specs=out_specs, check_vma=False
-    )
+        step, mesh=mesh, in_specs=in_specs, out_specs=out_specs, check_vma=False
+    )

time: 1500 us -> 749 us (0.50)
  waiting for transfers between devices: 720 us -> 404 us
  matrix products: 237 us -> 56.4 us
  blocking collectives: 217 us -> 56 us
  local copies, waits for them, and re-layouts: 179 us -> 70.5 us
  Pallas kernels: 0 us -> 71.3 us
  other arithmetic: 103 us -> 38.4 us
  starting transfers between devices: 8.18 us -> 30.9 us
    reduce_scatter x6 -> x3, waiting for transfers between devices: 489 us -> 113 us  [reduced(): lax.psum_scatter(both_slots.astype(BF16), LANE, scatter_dimension=0, tile...]
    dot_general x87 -> x21, matrix products: 237 us -> 56.4 us  [the longest x15 35.3 us: contract(): lax.dot_general(left, right, (((left_dim,), (right_dim,)), ((), ())), pre...]
    unnamed x15 -> x12, waiting for transfers between devices: 140 us -> 1.55 us
    unnamed x2 -> x0, blocking collectives: 123 us -> none
    all_gather x6 -> x7, waiting for transfers between devices: 82.2 us -> 190 us  [the longest x2 88.9 us: head_device(): lax.all_gather(pick(down_split, half, 0), LANE, axis=0, tiled=True)]
    pallas_call x0 -> x3, Pallas kernels: none -> 71.3 us  [the longest x1 33.7 us: attend_back(): pl.pallas_call(backward_kernel, grid_spec=pltpu.PrefetchScalarGridSpec(nu...]
    ppermute x0 -> x18, waiting for transfers between devices: none -> 68.5 us  [the longest x8 61.5 us: swap_slot(): return lax.ppermute(value, 'slot', SWAP)]
    dynamic_update_slice x24 -> x0, local copies, waits for them, and re-layouts: 59.5 us -> none  [the longest x16 39.8 us: value_pass(): lax.scan(value_per_key, jnp.zeros((heads_here, query_rows), jnp.float32),...]
  transfers between devices with their start and end apart: 16 -> 33, of which waited for: 9 -> 20; matrix products, arithmetic and copies ran while one was open for 16% -> 18% of each run, Pallas kernels for 0% -> 10%
where the time goes in v1:
time: 749 us; the launch traced here: 743 us
  waiting for transfers between devices  404 us (54%)
  Pallas kernels  71.3 us (10%)
  local copies, waits for them, and re-layouts  70.5 us (9%)
  matrix products  56.4 us (8%)
  blocking collectives  56 us (7%)
  other arithmetic  38.4 us (5%)
  starting transfers between devices  30.9 us (4%)
  between operations  15.9 us (2%)
    reduce_scatter x3, waiting for transfers between devices, reduced(): lax.psum_scatter(both_slots.astype(BF16), LANE, scatter_dimension=0, tile...  113 us
    all_gather x2, waiting for transfers between devices, head_device(): lax.all_gather(pick(down_split, half, 0), LANE, axis=0, tiled=True)  88.9 us
    all_gather x2, waiting for transfers between devices, head_device(): ups.append(lax.all_gather(up_part, LANE, axis=0, tiled=True))  71 us
    ppermute x8, waiting for transfers between devices, swap_slot(): return lax.ppermute(value, 'slot', SWAP)  61.5 us
    dot_general x15, matrix products, contract(): lax.dot_general(left, right, (((left_dim,), (right_dim,)), ((), ())), pre...  35.3 us
    all_gather x1, blocking collectives, head_device(): lax.all_gather(jnp.concatenate([w_proj, small], axis=0), GROUP, axis=0, t...  35.2 us
    pallas_call x1, Pallas kernels, attend_back(): pl.pallas_call(backward_kernel, grid_spec=pltpu.PrefetchScalarGridSpec(nu...  33.7 us
    all_gather x1, waiting for transfers between devices, head_device(): lax.all_gather(tokens, GROUP, axis=1, tiled=True)  30.2 us
  transfers between devices with their start and end apart: 33, of which 20 were waited for; matrix products, arithmetic and copies ran while one was open for 18% of the time, Pallas kernels for 10%

profile of v1, /device:TPU:0, one launch (start us, length us, event | category | flops | bytes accessed | tf_op | source)
XLA Modules:
  0.0 743.0 jit_solution(12798385199658147978)
XLA Ops:
  16.8 7.3 all-to-all-start
  24.3 35.2 %all-gather = bf16[1280,128]{1,0:T(8,128)(2,1)S(1)} all-gather(bf16[80,128]{1,0:T(8,128)(2,1)S(1)} %pad_maximum_fusion.7), channel_id=2, replica_groups=mesh['slot'=2,'ctx'=4,'x'=2,'core'=2] {'ctx','x','core'}, dimensions={0}, use_global_device_ids=true | all-gather | bytes 348160 | tf_op jit(solution)/shard_map/all_gather | solution.py:303
  68.9 30.2 %all-gather.11.cloned.1.call-done = bf16[2,2048,1024]{2,1,0:T(8,128)(2,1)} async-done(((bf16[2,128,1024]{2,1,0:T(8,128)(2,1)}), bf16[2,2048,1024]{2,1,0:T(8,128)(2,1)}) %all-gather.11.cloned.1.call-update) | async-done | bytes 8388624 | tf_op jit(solution)/shard_map/all_gather | solution.py:313
  99.1 11.1 %project.1 = (bf16[4096,64]{1,0:T(8,128)(2,1)}, bf16[4096,64]{1,0:T(8,128)(2,1)}, bf16[4096,64]{1,0:T(8,128)(2,1)}) custom-call(bf16[4096,1024]{1,0:T(8,128)(2,1)} %bitcast.203, bf16[1024,320]{1,0:T(8,128)(2,1)} %pad_maximum_fusion.3.w_ref, f32[1,320]{1,0:T(1,128)} %pad_maximum_fusion.10.b_ref, f32[2048,128]{1,0:T(8,128)} %copy.215.cos_ref, ...), custom_call_target="tpu_custom_call" | custom-call | flops 2684354560 | bytes 8388608 | tf_op jit(solution)/shard_map/project/pallas_call | solution.py:62
  110.1 26.5 %attend.1 = (f32[2,2048,64]{2,1,0:T(8,128)}, bf16[8,2,2,128,64]{4,3,2,1,0:T(8,128)(2,1)}, f32[2,1,2048]{2,1,0:T(1,128)}) custom-call(s32[2]{0:T(128)} %len_ref.3, s32[1]{0:T(128)} %bitcast.1.core_ref, bf16[2,2048,64]{2,1,0:T(8,128)(2,1)} %bitcast.270, bf16[2,2048,64]{2,1,0:T(8,128)(2,1)} %bitcast.272, bf16[2,2048,64]{2,1,0:T(8,128)(2,1)} %bitcast.274), custom_call_target="tpu_custom_call" | custom-call | flops 8589934592 | bytes 2097152 | tf_op jit(solution)/shard_map/attend/pallas_call | solution.py:134
  138.2 20.8 %all_to_all.25 = bf16[8,2,2,128,64]{3,4,2,1,0:T(8,128)(2,1)S(1)} all-to-all(bf16[8,2,2,128,64]{3,4,2,1,0:T(8,128)(2,1)S(1)} %copy.217), channel_id=1, replica_groups=mesh['slot'=2,'ctx'=4,'x'=2,'core'=2] {'ctx','x'}, dimensions={0} | all-to-all | bytes 1048576 | tf_op jit(solution)/shard_map/all_to_all | solution.py:366
  159.9 2.1 fusion.53
  168.5 24.7 %all-gather.17.cloned.1.call-done = bf16[1024,1024]{0,1:T(8,128)(2,1)} async-done(((bf16[128,1024]{0,1:T(8,128)(2,1)}), bf16[1024,1024]{0,1:T(8,128)(2,1)}) %all-gather.17.cloned.1.call-update) | async-done | bytes 2097168 | tf_op jit(solution)/shard_map/all_gather | solution.py:350
  193.2 4.9 multiply_convert_fusion
  198.1 44.4 %all-gather.23.cloned.1.call-done = bf16[1,1024,1024]{2,1,0:T(8,128)(2,1)} async-done(((bf16[1,128,1024]{2,1,0:T(8,128)(2,1)}), bf16[1,1024,1024]{2,1,0:T(8,128)(2,1)}) %all-gather.23.cloned.1.call-update) | async-done | bytes 2097168 | tf_op jit(solution)/shard_map/all_gather | solution.py:351
  242.5 4.6 fusion.14
  247.1 46.2 %all-gather.15.cloned.1.call-done = bf16[1024,1024]{0,1:T(8,128)(2,1)} async-done(((bf16[128,1024]{0,1:T(8,128)(2,1)}), bf16[1024,1024]{0,1:T(8,128)(2,1)}) %all-gather.15.cloned.1.call-update) | async-done | bytes 2097168 | tf_op jit(solution)/shard_map/all_gather | solution.py:350
  293.3 4.8 multiply_convert_fusion.1
  298.1 44.5 %all-gather.21.cloned.1.call-done = bf16[1,1024,1024]{2,1,0:T(8,128)(2,1)} async-done(((bf16[1,128,1024]{2,1,0:T(8,128)(2,1)}), bf16[1,1024,1024]{2,1,0:T(8,128)(2,1)}) %all-gather.21.cloned.1.call-update) | async-done | bytes 2097168 | tf_op jit(solution)/shard_map/all_gather | solution.py:351
  342.6 3.8 fusion.20
  356.0 2.7 convert_reduce_fusion.1
  361.4 2.7 convert_reduce_fusion
  370.8 2.1 multiply_reduce_fusion.2
  382.4 4.0 convolution_convert_fusion.1
  388.8 3.2 constant_dynamic-slice_fusion.1
  396.4 3.9 convolution_convert_fusion
  401.8 44.7 %collective-permute-done.10 = bf16[512,512]{1,0:T(8,128)(2,1)} collective-permute-done((bf16[512,512]{1,0:T(8,128)(2,1)}, bf16[512,512]{1,0:T(8,128)(2,1)}, u32[]{:S(2)}, u32[]{:S(2)}) %collective-permute-start.10) | collective-permute-done | bytes 524320 | tf_op jit(solution)/shard_map/ppermute | solution.py:38
  446.4 2.3 add_convert_fusion.5
  450.7 3.5 all-to-all-start.2
  454.5 2.6 fusion.43
  457.1 2.6 fusion.42
  459.8 3.9 add_convert_fusion.1
  463.7 17.3 %all-to-all-done.2 = bf16[8,2,2,128,64]{3,2,1,4,0:T(2,128)(2,1)S(1)} async-done(((bf16[8,2,2,128,64]{3,2,1,4,0:T(2,128)(2,1)}), bf16[8,2,2,128,64]{3,2,1,4,0:T(2,128)(2,1)S(1)}, u32[]{:S(2)}, u32[]{:S(2)}) %all-to-all-start.2) | async-done | bytes 524320 | tf_op jit(solution)/shard_map/all_to_all | solution.py:421
  485.2 33.7 %attend_back.1 = (f32[2,2048,64]{2,1,0:T(8,128)}, f32[2,2048,64]{2,1,0:T(8,128)}, f32[2,2048,64]{2,1,0:T(8,128)}) custom-call(s32[2]{0:T(128)} %len_ref.3, bf16[2,2048,64]{2,1,0:T(8,128)(2,1)} %bitcast.271, bf16[2,2048,64]{2,1,0:T(8,128)(2,1)} %bitcast.273, bf16[2,2048,64]{2,1,0:T(8,128)(2,1)} %bitcast.275, bf16[2,2048,64]{2,1,0:T(8,128)(2,1)} %bitcast.214, ...), custom_call_target="tpu_custom_call" | custom-call | flops 21474836480 | bytes 5242880 | tf_op jit(solution)/shard_map/attend_back/pallas_call | solution.py:211
  521.7 2.3 subtract_convert_fusion
  533.8 2.9 broadcast_select_fusion
  536.7 4.4 all-to-all-start.3
  541.4 3.9 add_convert_fusion
  545.3 5.5 concatenate.76
  551.4 5.2 fusion.29
  559.8 7.8 %collective-permute-done.9 = bf16[16,80,192]{2,1,0:T(8,128)(2,1)S(1)} collective-permute-done((bf16[16,80,192]{2,1,0:T(8,128)(2,1)S(1)}, bf16[16,80,192]{2,1,0:T(8,128)(2,1)S(1)}, u32[]{:S(2)}, u32[]{:S(2)}) %collective-permute-start.9) | collective-permute-done | bytes 491552 | tf_op jit(solution)/shard_map/ppermute | solution.py:38
  568.7 5.4 all-to-all-done.3
  574.0 3.6 all-to-all-start.4
  577.6 2.5 reshape.524
  580.2 3.7 fusion.55
  588.5 2.6 collective-permute-done.11
  592.8 7.9 %all-to-all-done.4 = bf16[16,80,192]{2,1,0:T(8,128)(2,1)S(1)} async-done(((bf16[16,80,192]{2,1,0:T(8,128)(2,1)}), bf16[16,80,192]{2,1,0:T(8,128)(2,1)S(1)}, u32[]{:S(2)}, u32[]{:S(2)}) %all-to-all-start.4) | async-done | bytes 491552 | tf_op jit(solution)/shard_map/all_to_all | solution.py:532
  603.0 2.8 reshape.530
  606.7 43.2 %reduce-scatter.9.cloned.1.call-done = bf16[128,1024]{1,0:T(8,128)(2,1)} async-done(((bf16[1024,1024]{1,0:T(8,128)(2,1)}), bf16[128,1024]{1,0:T(8,128)(2,1)}) %reduce-scatter.9.cloned.1.call-update) | async-done | bytes 262160 | tf_op jit(solution)/shard_map/reduce_scatter | solution.py:437
  651.1 69.9 %reduce-scatter.11.cloned.1.call-done = bf16[128,1024]{1,0:T(8,128)(2,1)} async-done(((bf16[1024,1024]{1,0:T(8,128)(2,1)}), bf16[128,1024]{1,0:T(8,128)(2,1)}) %reduce-scatter.11.cloned.1.call-update) | async-done | bytes 262160 | tf_op jit(solution)/shard_map/reduce_scatter | solution.py:437
  722.4 2.6 fusion.31
  725.7 3.9 collective-permute-done.17
  730.8 2.5 collective-permute-done.15
  (366 shorter events, 104.4 us)
Async XLA Ops:
  7.2 91.9 %all-gather.11.cloned.1.call-start = ((), (), s32[]{:S(2)}) async-start(), calls=%async_computation.9 | async-start | bytes 8912896 | tf_op jit(solution)/shard_map/all_gather | solution.py:313
  7.9 152.0 %all-gather.13.cloned.1.call-start = ((), (), s32[]{:S(2)}) async-start(), calls=%async_computation.10 | async-start | bytes 1179648 | tf_op jit(solution)/shard_map/all_gather | solution.py:341
  8.7 184.5 %all-gather.17.cloned.1.call-start = ((), (), s32[]{:S(2)}) async-start(), calls=%async_computation.12 | async-start | bytes 2359296 | tf_op jit(solution)/shard_map/all_gather | solution.py:350
  10.6 1.7 collective-permute-start.2
  13.3 229.1 %all-gather.23.cloned.1.call-start = ((), (), s32[]{:S(2)}) async-start(), calls=%async_computation.18 | async-start | bytes 2359296 | tf_op jit(solution)/shard_map/all_gather | solution.py:351
  14.8 9.4 %copy-start.48 = (bf16[192]{0:T(256)(128)(2,1)S(1)}, bf16[192]{0:T(256)(128)(2,1)}, u32[]{:S(2)}) copy-start(bf16[192]{0:T(256)(128)(2,1)} %param.20) | copy-start | bytes 1156
  14.8 9.4 %copy-start.49 = (bf16[64]{0:T(256)(128)(2,1)S(1)}, bf16[64]{0:T(256)(128)(2,1)}, u32[]{:S(2)}) copy-start(bf16[64]{0:T(256)(128)(2,1)} %param.22) | copy-start | bytes 388
  14.8 9.4 %copy-start.50 = (bf16[64]{0:T(256)(128)(2,1)S(1)}, bf16[64]{0:T(256)(128)(2,1)}, u32[]{:S(2)}) copy-start(bf16[64]{0:T(256)(128)(2,1)} %param.23) | copy-start | bytes 388
  14.8 9.4 %copy-start.51 = (bf16[64]{0:T(256)(128)(2,1)S(1)}, bf16[64]{0:T(256)(128)(2,1)}, u32[]{:S(2)}) copy-start(bf16[64]{0:T(256)(128)(2,1)} %param.24) | copy-start | bytes 388
  14.8 9.4 %copy-start.52 = (bf16[256]{0:T(256)(128)(2,1)S(1)}, bf16[256]{0:T(256)(128)(2,1)}, u32[]{:S(2)}) copy-start(bf16[256]{0:T(256)(128)(2,1)} %param.26) | copy-start | bytes 1540
  14.9 9.4 %copy-start.41 = (bf16[64,128]{1,0:T(8,128)(2,1)S(1)}, bf16[64,128]{1,0:T(8,128)(2,1)}, u32[]{:S(2)}) copy-start(bf16[64,128]{1,0:T(8,128)(2,1)} %param.31) | copy-start | bytes 49156
  16.8 49.3 %all-to-all-start = ((bf16[16,64,192]{2,1,0:T(8,128)(2,1)}), bf16[16,64,192]{2,1,0:T(8,128)(2,1)S(1)}, u32[]{:S(2)}, u32[]{:S(2)}) async-start(bf16[16,64,192]{2,1,0:T(8,128)(2,1)} %copy.210), calls=%async_computation | async-start | bytes 1048576 | tf_op jit(solution)/shard_map/all_to_all | solution.py:311
  24.1 269.2 %all-gather.15.cloned.1.call-start = ((), (), s32[]{:S(2)}) async-start(), calls=%async_computation.11 | async-start | bytes 2359296 | tf_op jit(solution)/shard_map/all_gather | solution.py:350
  61.6 281.0 %all-gather.21.cloned.1.call-start = ((), (), s32[]{:S(2)}) async-start(), calls=%async_computation.17 | async-start | bytes 2359296 | tf_op jit(solution)/shard_map/all_gather | solution.py:351
  163.0 3.0 collective-permute-start
  163.1 394.0 %reduce-scatter.13.cloned.1.call-start = ((), (), s32[]{:S(2)}) async-start(), calls=%async_computation.19 | async-start | bytes 626688
  168.2 125.1 %copy-start.29 = (bf16[256,1024]{1,0:T(8,128)(2,1)}, bf16[256,1024]{1,0:T(8,128)(2,1)S(1)}, u32[]{:S(2)}) copy-start(bf16[256,1024]{1,0:T(8,128)(2,1)S(1)} %fusion.37) | copy-start | bytes 1572868
  168.2 25.0 %collective-permute-start.1 = (bf16[256,1024]{1,0:T(8,128)(2,1)S(1)}, bf16[256,1024]{1,0:T(8,128)(2,1)S(1)}, u32[]{:S(2)}, u32[]{:S(2)}) collective-permute-start(bf16[256,1024]{1,0:T(8,128)(2,1)S(1)} %fusion.37), channel_id=1, source_target_pairs={{0,1},{1,0},{2,3},{3,2},{4,5},{5,4},{6,7},{7,6},{8,9},{9,8},{10,11... | collective-permute-start | bytes 1572872 | tf_op jit(solution)/shard_map/ppermute | solution.py:34
  168.5 29.7 %copy-start.44 = (f32[8,1,1,128]{3,2,1,0:T(1,128)}, f32[8,1,1,128]{3,2,1,0:T(1,128)S(1)}, u32[]{:S(2)}) copy-start(f32[8,1,1,128]{3,2,1,0:T(1,128)S(1)} %get-tuple-element.82) | copy-start | bytes 12292
  168.5 124.8 %copy-start.46 = (f32[8,1,1,128]{3,2,1,0:T(1,128)}, f32[8,1,1,128]{3,2,1,0:T(1,128)S(1)}, u32[]{:S(2)}) copy-start(f32[8,1,1,128]{3,2,1,0:T(1,128)S(1)} %get-tuple-element.81) | copy-start | bytes 12292
  193.2 100.1 %copy-start.61 = (bf16[256,1024]{1,0:T(8,128)(2,1)}, bf16[256,1024]{1,0:T(8,128)(2,1)S(1)}, u32[]{:S(2)}) copy-start(bf16[256,1024]{1,0:T(8,128)(2,1)S(1)} %collective-permute-done.1) | copy-start | bytes 1572868
  347.5 3.0 collective-permute-start.3
  353.9 14.6 %copy-start.4 = (bf16[256,1024]{1,0:T(8,128)(2,1)}, bf16[256,1024]{1,0:T(8,128)(2,1)S(1)}, u32[]{:S(2)}) copy-start(bf16[256,1024]{1,0:T(8,128)(2,1)S(1)} %get-tuple-element.59) | copy-start | bytes 1572868
  353.9 2.1 collective-permute-start.4
  367.8 3.1 collective-permute-start.5
  375.6 204.6 %all-gather.19.cloned.1.call-start = ((), (), s32[]{:S(2)}) async-start(), calls=%async_computation.13 | async-start | bytes 3538944 | tf_op jit(solution)/shard_map/all_gather | solution.py:359
  377.8 1.8 collective-permute-start.7
  381.9 204.6 %reduce-scatter.7.cloned.1.call-start = ((), (), s32[]{:S(2)}) async-start(), calls=%async_computation.14 | async-start | bytes 589824 | tf_op jit(solution)/shard_map/reduce_scatter | solution.py:437
  381.9 5.9 collective-permute-start.6
  386.4 73.4 %collective-permute-start.13 = (bf16[1024,1024]{1,0:T(8,128)(2,1)}, bf16[1024,1024]{1,0:T(8,128)(2,1)}, u32[]{:S(2)}, u32[]{:S(2)}) collective-permute-start(bf16[1024,1024]{1,0:T(8,128)(2,1)} %convolution_convert_fusion.1), channel_id=1, source_target_pairs={{0,16},{16,0},{1,17},{17,1},{2,18},{18,2},{3,19},{19,3},{4,20},{20... | collective-permute-start | bytes 6291464 | tf_op jit(solution)/shard_map/ppermute | solution.py:38
  393.2 53.3 %collective-permute-start.10 = (bf16[512,512]{1,0:T(8,128)(2,1)}, bf16[512,512]{1,0:T(8,128)(2,1)}, u32[]{:S(2)}, u32[]{:S(2)}) collective-permute-start(bf16[512,512]{1,0:T(8,128)(2,1)} %convolution_convert_fusion.2), channel_id=1, source_target_pairs={{0,16},{16,0},{1,17},{17,1},{2,18},{18,2},{3,19},{19,3},{4,20},{20... | collective-permute-start | bytes 1572872 | tf_op jit(solution)/shard_map/ppermute | solution.py:38
  396.4 50.0 %copy-start.23 = (bf16[512,1,512]{2,1,0:T(2,128)(2,1)S(1)}, bf16[512,1,512]{2,1,0:T(2,128)(2,1)}, u32[]{:S(2)}) copy-start(bf16[512,1,512]{2,1,0:T(2,128)(2,1)} %get-tuple-element.60) | copy-start | bytes 1572868
  400.3 48.4 %copy-start.22 = (bf16[512,1024]{1,0:T(8,128)(2,1)S(1)}, bf16[512,1024]{1,0:T(8,128)(2,1)}, u32[]{:S(2)}) copy-start(bf16[512,1024]{1,0:T(8,128)(2,1)} %all-gather.13.cloned.1.call-done) | copy-start | bytes 3145732
  400.3 141.1 %collective-permute-start.16 = (bf16[1024,1024]{1,0:T(8,128)(2,1)}, bf16[1024,1024]{1,0:T(8,128)(2,1)}, u32[]{:S(2)}, u32[]{:S(2)}) collective-permute-start(bf16[1024,1024]{1,0:T(8,128)(2,1)} %convolution_convert_fusion), channel_id=1, source_target_pairs={{0,16},{16,0},{1,17},{17,1},{2,18},{18,2},{3,19},{19,3},{4,20},{20... | collective-permute-start | bytes 6291464 | tf_op jit(solution)/shard_map/ppermute | solution.py:38
  450.7 30.3 %all-to-all-start.2 = ((bf16[8,2,2,128,64]{3,2,1,4,0:T(2,128)(2,1)}), bf16[8,2,2,128,64]{3,2,1,4,0:T(2,128)(2,1)S(1)}, u32[]{:S(2)}, u32[]{:S(2)}) async-start(bf16[8,2,2,128,64]{3,2,1,4,0:T(2,128)(2,1)} %bitcast.36), calls=%async_computation.2 | async-start | bytes 1048576 | tf_op jit(solution)/shard_map/all_to_all | solution.py:421
  454.2 195.7 %reduce-scatter.9.cloned.1.call-start = ((), (), s32[]{:S(2)}) async-start(), calls=%async_computation.15 | async-start | bytes 2359296 | tf_op jit(solution)/shard_map/reduce_scatter | solution.py:437
  463.7 20.3 %copy-start.17 = (f32[2,2048,64]{2,1,0:T(8,128)S(1)}, f32[2,2048,64]{2,1,0:T(8,128)}, u32[]{:S(2)}) copy-start(f32[2,2048,64]{2,1,0:T(8,128)} %get-tuple-element.30) | copy-start | bytes 3145732
  536.7 37.4 %all-to-all-start.3 = ((bf16[8,2,2,128,192]{3,2,1,4,0:T(2,128)(2,1)}), bf16[8,2,2,128,192]{3,2,1,4,0:T(2,128)(2,1)}, u32[]{:S(2)}, u32[]{:S(2)}) async-start(bf16[8,2,2,128,192]{3,2,1,4,0:T(2,128)(2,1)} %broadcast_select_fusion), calls=%async_computation.3 | async-start | bytes 3145728 | tf_op jit(solution)/shard_map/all_to_all | solution.py:540
  541.1 179.9 %reduce-scatter.11.cloned.1.call-start = ((), (), s32[]{:S(2)}) async-start(), calls=%async_computation.16 | async-start | bytes 2359296 | tf_op jit(solution)/shard_map/reduce_scatter | solution.py:437
  557.0 10.7 %collective-permute-start.9 = (bf16[16,80,192]{2,1,0:T(8,128)(2,1)S(1)}, bf16[16,80,192]{2,1,0:T(8,128)(2,1)S(1)}, u32[]{:S(2)}, u32[]{:S(2)}) collective-permute-start(bf16[16,80,192]{2,1,0:T(8,128)(2,1)S(1)} %pad_maximum_fusion.4), channel_id=1, source_target_pairs={{0,16},{16,0},{1,17},{17,1},{2,18},{18,2},{3,19},{19,3},{4,20},{20... | collective-permute-start | bytes 1474568 | tf_op jit(solution)/shard_map/ppermute | solution.py:38
  557.9 28.6 %collective-permute-start.12 = (bf16[72,128]{1,0:T(8,128)(2,1)S(1)}, bf16[72,128]{1,0:T(8,128)(2,1)S(1)}, u32[]{:S(2)}, u32[]{:S(2)}) collective-permute-start(bf16[72,128]{1,0:T(8,128)(2,1)S(1)} %convert_element_type.222), channel_id=1, source_target_pairs={{0,16},{16,0},{1,17},{17,1},{2,18},{18,2},{3,19},{19,3},{4,20},{20... | collective-permute-start | bytes 55304 | tf_op jit(solution)/shard_map/ppermute | solution.py:38
  574.0 26.6 %all-to-all-start.4 = ((bf16[16,80,192]{2,1,0:T(8,128)(2,1)}), bf16[16,80,192]{2,1,0:T(8,128)(2,1)S(1)}, u32[]{:S(2)}, u32[]{:S(2)}) async-start(bf16[16,80,192]{2,1,0:T(8,128)(2,1)} %add_convert_fusion.4), calls=%async_computation.4 | async-start | bytes 1310720 | tf_op jit(solution)/shard_map/all_to_all | solution.py:532
  584.9 137.5 %collective-permute-start.8 = (f32[256,1024]{1,0:T(8,128)}, f32[256,1024]{1,0:T(8,128)}, u32[]{:S(2)}, u32[]{:S(2)}) collective-permute-start(f32[256,1024]{1,0:T(8,128)} %slice.191), channel_id=1, source_target_pairs={{0,1},{1,0},{2,3},{3,2},{4,5},{5,4},{6,7},{7,6},{8,9},{9,8},{10,11... | collective-permute-start | bytes 3145736 | tf_op jit(solution)/shard_map/ppermute | solution.py:34
  586.5 4.6 collective-permute-start.11
  605.8 116.7 %copy-start.9 = (f32[256,1024]{1,0:T(8,128)S(1)}, f32[256,1024]{1,0:T(8,128)}, u32[]{:S(2)}) copy-start(f32[256,1024]{1,0:T(8,128)} %get-tuple-element.47) | copy-start | bytes 3145732
  651.0 74.0 %collective-permute-start.14 = (bf16[64,8,128]{2,1,0:T(8,128)(2,1)S(1)}, bf16[64,8,128]{2,1,0:T(8,128)(2,1)S(1)}, u32[]{:S(2)}, u32[]{:S(2)}) collective-permute-start(bf16[64,8,128]{2,1,0:T(8,128)(2,1)S(1)} %get-tuple-element.72), channel_id=1, source_target_pairs={{0,1},{1,0},{2,3},{3,2},{4,5},{5,4},{6,7},{7,6},{8,9},{9,8},{10,11... | collective-permute-start | bytes 393224 | tf_op jit(solution)/shard_map/ppermute | solution.py:34
  721.0 8.6 %collective-permute-start.17 = (bf16[128,1024]{1,0:T(8,128)(2,1)}, bf16[128,1024]{1,0:T(8,128)(2,1)S(1)}, u32[]{:S(2)}, u32[]{:S(2)}) collective-permute-start(bf16[128,1024]{1,0:T(8,128)(2,1)} %reduce-scatter.11.cloned.1.call-done), channel_id=1, source_target_pairs={{0,16},{16,0},{1,17},{17,1},{2,18},{18,2},{3,19},{19,3},{4,20},{20... | collective-permute-start | bytes 786440 | tf_op jit(solution)/shard_map/ppermute | solution.py:38
  725.1 8.2 %collective-permute-start.15 = (bf16[64,8,2,128]{3,1,0,2:T(8,128)(2,1)S(1)}, bf16[64,8,2,128]{3,1,0,2:T(8,128)(2,1)S(1)}, u32[]{:S(2)}, u32[]{:S(2)}) collective-permute-start(bf16[64,8,2,128]{3,1,0,2:T(8,128)(2,1)S(1)} %maximum_select_fusion.5), channel_id=1, source_target_pairs={{0,16},{16,0},{1,17},{17,1},{2,18},{18,2},{3,19},{19,3},{4,20},{20... | collective-permute-start | bytes 786440 | tf_op jit(solution)/shard_map/ppermute | solution.py:38
  (57 other events, 184.2 us)
Sparse Core Ops, SparseCore 0:
  10.2 88.8 all-gather.10
  101.2 38.9 all-gather.12
  142.8 50.3 all-gather.16
  195.2 47.2 all-gather.22
  244.4 48.8 all-gather.14
  295.3 47.2 all-gather.20
  375.7 52.6 reduce-scatter.12
  430.4 65.1 all-gather.18
  498.9 74.4 reduce-scatter.6
  576.8 73.0 reduce-scatter.8
  653.5 67.4 reduce-scatter.10

commit v2 on v1

--- a/solution.py
+++ b/solution.py
@@ -344,13 +344,11 @@
     up_theirs = swap_core(pick(up_split, 1 - core, 2))
     up_chip = two_lanes(up_mine, up_theirs).reshape(2 * shard, n_lane, 2, ff_half)
     down_split = w_down.reshape(2, ff_half, width)
-    ups, downs = [], []
-    for half in (slot, 1 - slot):
-        up_part = pick(up_chip, half, 2).reshape(2 * shard, n_lane * ff_half)
-        ups.append(lax.all_gather(up_part, LANE, axis=0, tiled=True))
-        downs.append(lax.all_gather(pick(down_split, half, 0), LANE, axis=0, tiled=True))
+    up_part = pick(up_chip, slot, 2).reshape(2 * shard, n_lane * ff_half)
+    up = lax.all_gather(up_part, LANE, axis=0, tiled=True)
+    down = lax.all_gather(pick(down_split, slot, 0), LANE, axis=0, tiled=True)
     bias_lane = pick(up_bias.reshape(n_lane, 2, 2, ff_half), core, 1)
-    up_biases = [pick(bias_lane, half, 1).reshape(-1) for half in (slot, 1 - slot)]
+    up_bias_own = pick(bias_lane, slot, 1).reshape(-1)
 
     qkv_split = w_qkv.reshape(shard, 3, n_lane, 2, HD)
     qkv_mine = pick(qkv_split, core, 3)
@@ -372,21 +370,22 @@
     def both(value):
         return jnp.concatenate([value, swap_core(value)], axis=0)
 
+    def quad(value):
+        pair = jnp.concatenate([value, swap_slot(value)], axis=0)
+        return jnp.concatenate([pair, swap_core(pair)], axis=0)
+
+    def quad_sum(partial_rows):
+        pair = partial_rows[: 2 * rows] + swap_core(partial_rows[2 * rows :])
+        return pair[:rows] + swap_slot(pair[rows:].astype(BF16)).astype(F32)
+
     flat_tokens = tokens.reshape(rows, width).astype(F32)
     attended = own_sum(mm(merged, out_lane)) + out_bias
     hidden_one, unit_one, root_one = norm_forward(flat_tokens + attended, gain_one, shift_one)
-    hidden_low = both(hidden_one.astype(BF16))
-
-    actives, slopes = [], []
-    downward = None
-    for up, bias, down in zip(ups, up_biases, downs):
-        active, slope = gelu_pair(mm(hidden_low, up) + bias)
-        active = active.astype(BF16)
-        actives.append(active)
-        slopes.append(slope)
-        term = mm(active, down)
-        downward = term if downward is None else downward + term
-    downward = own_sum(downward) + down_bias
+    hidden_low = quad(hidden_one.astype(BF16))
+
+    active, slope = gelu_pair(mm(hidden_low, up) + up_bias_own)
+    active = active.astype(BF16)
+    downward = quad_sum(mm(active, down)) + down_bias
     out_rows, unit_two, root_two = norm_forward(hidden_one + downward, gain_two, shift_two)
     out_low = out_rows.astype(BF16)
     embeds = mm(out_low, proj_full).astype(BF16)
@@ -400,18 +399,12 @@
     grad_two, d_gain_two, d_shift_two = norm_backward(grad_full, unit_two, root_two, gain_two)
     grad_down_own = grad_two.astype(BF16)
     d_down_bias = jnp.sum(grad_down_own.astype(F32), axis=0)
-    grad_down = both(grad_down_own)
-
-    d_ups, d_downs, d_up_biases = [], [], []
-    grad_hidden = None
-    for up, down, active, slope in zip(ups, downs, actives, slopes):
-        grad_up = (contract(grad_down, down, 1, 1) * slope).astype(BF16)
-        d_downs.append(contract(active, grad_down, 0, 0).astype(BF16))
-        d_ups.append(contract(hidden_low, grad_up, 0, 0).astype(BF16))
-        d_up_biases.append(jnp.sum(grad_up.astype(F32), axis=0))
-        term = contract(grad_up, up, 1, 1)
-        grad_hidden = term if grad_hidden is None else grad_hidden + term
-    grad_hidden = grad_two + own_sum(grad_hidden)
+    grad_down = quad(grad_down_own)
+    grad_up = (contract(grad_down, down, 1, 1) * slope).astype(BF16)
+    d_down = contract(active, grad_down, 0, 0).astype(BF16)
+    d_up = contract(hidden_low, grad_up, 0, 0).astype(BF16)
+    up_bias_own_grad = jnp.sum(grad_up.astype(F32), axis=0)
+    grad_hidden = grad_two + quad_sum(contract(grad_up, up, 1, 1))
     grad_one, d_gain_one, d_shift_one = norm_backward(grad_hidden, unit_one, root_one, gain_one)
     grad_att_own = grad_one.astype(BF16)
     d_out_bias = jnp.sum(grad_att_own.astype(F32), axis=0)
@@ -436,8 +429,8 @@
         both_slots = pair[0].astype(F32) + swap_slot(pair[1]).astype(F32)
         return lax.psum_scatter(both_slots.astype(BF16), LANE, scatter_dimension=0, tiled=True)
 
-    red_down = reduced(d_downs)
-    red_up = reduced(d_ups)
+    red_down = lax.psum_scatter(d_down, LANE, scatter_dimension=0, tiled=True)
+    red_up = lax.psum_scatter(d_up, LANE, scatter_dimension=0, tiled=True)
     red_out = reduced(d_outs)
 
     def halves(mine, axis):
@@ -456,15 +449,10 @@
     )
     grad_w_up = halves(up_lanes, 3).reshape(shard, w_up.shape[1]).astype(F32)
 
-    up_bias_grad = jnp.stack(d_up_biases, axis=0)
-    up_bias_grad = jnp.where(slot == 0, up_bias_grad, jnp.flip(up_bias_grad, axis=0))
-    up_bias_grad = up_bias_grad.reshape(2, n_lane, ff_half).transpose(1, 0, 2)
-    zero_lane = jnp.zeros_like(up_bias_grad)
-    up_bias_grad = jnp.where(
-        core == 0,
-        jnp.stack([up_bias_grad, zero_lane], 1),
-        jnp.stack([zero_lane, up_bias_grad], 1),
-    )
+    spread = (
+        (jnp.arange(2) == core)[:, None, None] & (jnp.arange(2) == slot)[None, :, None]
+    ).astype(F32)
+    up_bias_grad = up_bias_own_grad.reshape(n_lane, 1, 1, ff_half) * spread[None]
     vectors = (
         d_out_bias,
         d_gain_one,

time: 749 us -> 717 us (0.957)
  waiting for transfers between devices: 404 us -> 354 us
  starting transfers between devices: 30.9 us -> 41.8 us
    all_gather x4 -> x2, waiting for transfers between devices: 160 us -> 51 us  [the longest x1 42.8 us: head_device(): down = lax.all_gather(pick(down_split, slot, 0), LANE, axis=0, tiled=True)]
    reduce_scatter x0 -> x2, waiting for transfers between devices: none -> 85.4 us  [the longest x1 68.4 us: head_device(): red_down = lax.psum_scatter(d_down, LANE, scatter_dimension=0, tiled=True)]
    all_gather x1, waiting for transfers between devices: 0.02 us -> 62.6 us  [head_device(): lax.all_gather(qkv_chip.reshape(2 * shard, n_lane * head_cols), LANE, axi...]
    reduce_scatter x3 -> x1, waiting for transfers between devices: 113 us -> 57.2 us  [reduced(): lax.psum_scatter(both_slots.astype(BF16), LANE, scatter_dimension=0, tile...]
    all_to_all x1, waiting for transfers between devices: 17.3 us -> 0.01 us  [head_device(): grad_heads = lax.all_to_all(grad_merged, LANE, 0, 0, tiled=True)]
    ppermute x8 -> x10, waiting for transfers between devices: 61.5 us -> 47.9 us  [swap_slot(): return lax.ppermute(value, 'slot', SWAP)]
    all_gather x1, starting transfers between devices: 0.04 us -> 8.69 us  [head_device(): lax.all_gather(qkv_chip.reshape(2 * shard, n_lane * head_cols), LANE, axi...]
    ppermute x10, waiting for transfers between devices: 6.99 us -> 15 us  [swap_core(): return lax.ppermute(value, 'core', SWAP)]
  transfers between devices with their start and end apart: 33 -> 33, of which waited for: 20 -> 18; matrix products, arithmetic and copies ran while one was open for 18% -> 18% of each run, Pallas kernels for 10% -> 10%
where the time goes in v2:
time: 717 us; the launch traced here: 704 us
  waiting for transfers between devices  354 us (49%)
  local copies, waits for them, and re-layouts  76.9 us (11%)
  Pallas kernels  71.2 us (10%)
  blocking collectives  54.4 us (8%)
  matrix products  50.6 us (7%)
  starting transfers between devices  41.8 us (6%)
  other arithmetic  39.7 us (6%)
  between operations  15.7 us (2%)
    reduce_scatter x1, waiting for transfers between devices, head_device(): red_down = lax.psum_scatter(d_down, LANE, scatter_dimension=0, tiled=True)  68.4 us
    all_gather x1, waiting for transfers between devices, head_device(): lax.all_gather(qkv_chip.reshape(2 * shard, n_lane * head_cols), LANE, axi...  62.6 us
    reduce_scatter x1, waiting for transfers between devices, reduced(): lax.psum_scatter(both_slots.astype(BF16), LANE, scatter_dimension=0, tile...  57.2 us
    ppermute x10, waiting for transfers between devices, swap_slot(): return lax.ppermute(value, 'slot', SWAP)  47.9 us
    all_gather x1, waiting for transfers between devices, head_device(): down = lax.all_gather(pick(down_split, slot, 0), LANE, axis=0, tiled=True)  42.8 us
    dot_general x11, matrix products, contract(): lax.dot_general(left, right, (((left_dim,), (right_dim,)), ((), ())), pre...  35.9 us
    all_gather x1, blocking collectives, head_device(): lax.all_gather(jnp.concatenate([w_proj, small], axis=0), GROUP, axis=0, t...  33.7 us
    pallas_call x1, Pallas kernels, attend_back(): pl.pallas_call(backward_kernel, grid_spec=pltpu.PrefetchScalarGridSpec(nu...  33.6 us
  transfers between devices with their start and end apart: 33, of which 18 were waited for; matrix products, arithmetic and copies ran while one was open for 18% of the time, Pallas kernels for 10%

profile of v2, /device:TPU:0, one launch (start us, length us, event | category | flops | bytes accessed | tf_op | source)
XLA Modules:
  0.0 704.0 jit_solution(2267404977641668219)
XLA Ops:
  12.9 7.0 all-to-all-start
  20.9 33.7 %all-gather = bf16[1280,128]{1,0:T(8,128)(2,1)S(1)} all-gather(bf16[80,128]{1,0:T(8,128)(2,1)S(1)} %pad_maximum_fusion.13), channel_id=2, replica_groups=mesh['slot'=2,'ctx'=4,'x'=2,'core'=2] {'ctx','x','core'}, dimensions={0}, use_global_device_ids=true | all-gather | bytes 348160 | tf_op jit(solution)/shard_map/all_gather | solution.py:303
  65.3 33.0 %all-gather.8.cloned.1.call-done = bf16[2,2048,1024]{2,1,0:T(8,128)(2,1)} async-done(((bf16[2,128,1024]{2,1,0:T(8,128)(2,1)}), bf16[2,2048,1024]{2,1,0:T(8,128)(2,1)}) %all-gather.8.cloned.1.call-update) | async-done | bytes 8388624 | tf_op jit(solution)/shard_map/all_gather | solution.py:313
  98.3 11.1 %project.1 = (bf16[4096,64]{1,0:T(8,128)(2,1)}, bf16[4096,64]{1,0:T(8,128)(2,1)}, bf16[4096,64]{1,0:T(8,128)(2,1)}) custom-call(bf16[4096,1024]{1,0:T(8,128)(2,1)} %bitcast.176, bf16[1024,320]{1,0:T(8,128)(2,1)} %pad_maximum_fusion.9.w_ref, f32[1,320]{1,0:T(1,128)} %pad_maximum_fusion.15.b_ref, f32[2048,128]{1,0:T(8,128)} %copy.211.cos_ref, ...), custom_call_target="tpu_custom_call" | custom-call | flops 2684354560 | bytes 8388608 | tf_op jit(solution)/shard_map/project/pallas_call | solution.py:62
  109.4 26.5 %attend.1 = (f32[2,2048,64]{2,1,0:T(8,128)}, bf16[8,2,2,128,64]{4,3,2,1,0:T(8,128)(2,1)}, f32[2,1,2048]{2,1,0:T(1,128)}) custom-call(s32[2]{0:T(128)} %len_ref.3, s32[1]{0:T(128)} %bitcast.1.core_ref, bf16[2,2048,64]{2,1,0:T(8,128)(2,1)} %bitcast.235, bf16[2,2048,64]{2,1,0:T(8,128)(2,1)} %bitcast.237, bf16[2,2048,64]{2,1,0:T(8,128)(2,1)} %bitcast.239), custom_call_target="tpu_custom_call" | custom-call | flops 8589934592 | bytes 2097152 | tf_op jit(solution)/shard_map/attend/pallas_call | solution.py:134
  137.5 20.8 %all_to_all.25 = bf16[8,2,2,128,64]{3,4,2,1,0:T(8,128)(2,1)S(1)} all-to-all(bf16[8,2,2,128,64]{3,4,2,1,0:T(8,128)(2,1)S(1)} %copy.213), channel_id=1, replica_groups=mesh['slot'=2,'ctx'=4,'x'=2,'core'=2] {'ctx','x'}, dimensions={0} | all-to-all | bytes 1048576 | tf_op jit(solution)/shard_map/all_to_all | solution.py:364
  159.1 2.1 fusion.36
  169.1 14.0 %collective-permute-done.1 = bf16[256,1024]{1,0:T(8,128)(2,1)S(1)} collective-permute-done((bf16[256,1024]{1,0:T(8,128)(2,1)S(1)}, bf16[256,1024]{1,0:T(8,128)(2,1)S(1)}, u32[]{:S(2)}, u32[]{:S(2)}) %collective-permute-start.1) | collective-permute-done | bytes 524320 | tf_op jit(solution)/shard_map/ppermute | solution.py:38
  184.2 8.3 %all-gather.12.cloned.1.call-done = bf16[1024,1024]{0,1:T(8,128)(2,1)} async-done(((bf16[128,1024]{0,1:T(8,128)(2,1)}), bf16[1024,1024]{0,1:T(8,128)(2,1)}) %all-gather.12.cloned.1.call-update) | async-done | bytes 2097168 | tf_op jit(solution)/shard_map/all_gather | solution.py:348
  192.5 7.1 %multiply_convert_fusion = (bf16[1024,1024]{1,0:T(8,128)(2,1)}, f32[1024,1024]{1,0:T(8,128)}) fusion(f32[1024]{0:T(1024)S(1)} %bitcast.232, bf16[1024,1024]{0,1:T(8,128)(2,1)} %all-gather.12.cloned.1.call-done, bf16[512,1024]{1,0:T(8,128)(2,1)} %collective-permute-done.2, bf16[256,1024]{1,0:T(8,128)(2,1)S(1)} %collective-permute-done.1, ...), kind=kOutput, calls=%fused_computation.8 | convolution fusion | flops 2160066560 | bytes 10489856 | tf_op jit(solution)/shard_map/dot_general | solution.py:24
  199.6 42.8 %all-gather.16.cloned.1.call-done = bf16[1,1024,1024]{2,1,0:T(8,128)(2,1)} async-done(((bf16[1,128,1024]{2,1,0:T(8,128)(2,1)}), bf16[1,1024,1024]{2,1,0:T(8,128)(2,1)}) %all-gather.16.cloned.1.call-update) | async-done | bytes 2097168 | tf_op jit(solution)/shard_map/all_gather | solution.py:349
  242.3 4.5 fusion.7
  249.6 4.5 collective-permute-done.4
  254.1 2.6 slice_add_fusion.1
  260.7 11.4 %collective-permute-done.5 = bf16[256,1024]{1,0:T(8,128)(2,1)S(1)} collective-permute-done((bf16[256,1024]{1,0:T(8,128)(2,1)S(1)}, bf16[256,1024]{1,0:T(8,128)(2,1)S(1)}, u32[]{:S(2)}, u32[]{:S(2)}) %collective-permute-start.5) | collective-permute-done | bytes 524320 | tf_op jit(solution)/shard_map/ppermute | solution.py:38
  276.9 11.6 %collective-permute-done.6 = bf16[256,1024]{1,0:T(8,128)(2,1)S(1)} collective-permute-done((bf16[256,1024]{1,0:T(8,128)(2,1)S(1)}, bf16[256,1024]{1,0:T(8,128)(2,1)S(1)}, u32[]{:S(2)}, u32[]{:S(2)}) %collective-permute-start.6) | collective-permute-done | bytes 524320 | tf_op jit(solution)/shard_map/ppermute | solution.py:38
  288.7 2.6 collective-permute-done.7
  291.4 6.5 convert_reduce_fusion
  298.0 2.3 fusion.37
  300.8 4.0 collective-permute-done.8
  311.8 10.1 %collective-permute-done.9 = bf16[256,1024]{1,0:T(8,128)(2,1)} collective-permute-done((bf16[256,1024]{1,0:T(8,128)(2,1)}, bf16[256,1024]{1,0:T(8,128)(2,1)}, u32[]{:S(2)}, u32[]{:S(2)}) %collective-permute-start.9) | collective-permute-done | bytes 524320 | tf_op jit(solution)/shard_map/ppermute | solution.py:38
  322.0 2.0 multiply_reduce_fusion.2
  326.6 5.7 convolution_convert_fusion.1
  333.9 5.3 convolution_convert_fusion
  345.8 3.5 all-to-all-start.2
  349.3 8.7 %all-gather.14.cloned.1.call-start = ((), (), s32[]{:S(2)}) async-start(), calls=%async_computation.12 | async-start | bytes 3538944 | tf_op jit(solution)/shard_map/all_gather | solution.py:357
  368.6 2.6 multiply_reduce_fusion
  371.8 33.6 %attend_back.1 = (f32[2,2048,64]{2,1,0:T(8,128)}, f32[2,2048,64]{2,1,0:T(8,128)}, f32[2,2048,64]{2,1,0:T(8,128)}) custom-call(s32[2]{0:T(128)} %len_ref.3, bf16[2,2048,64]{2,1,0:T(8,128)(2,1)} %bitcast.236, bf16[2,2048,64]{2,1,0:T(8,128)(2,1)} %bitcast.238, bf16[2,2048,64]{2,1,0:T(8,128)(2,1)} %bitcast.240, bf16[2,2048,64]{2,1,0:T(8,128)(2,1)} %bitcast.187, ...), custom_call_target="tpu_custom_call" | custom-call | flops 21474836480 | bytes 5242880 | tf_op jit(solution)/shard_map/attend_back/pallas_call | solution.py:211
  408.4 2.5 subtract_convert_fusion
  410.9 2.8 copy.222
  413.7 2.1 copy.223
  421.4 2.8 broadcast_select_fusion
  424.1 5.6 all-to-all-start.3
  431.8 3.2 constant_dynamic-slice_fusion.1
  437.0 2.0 collective-permute-start.14
  440.3 5.8 concatenate.86
  446.1 5.4 fusion.11
  454.4 2.3 add_convert_fusion.3
  456.7 17.0 %reduce-scatter.9.cloned.1.call-done = bf16[128,1024]{1,0:T(8,128)(2,1)} async-done(((bf16[1024,1024]{1,0:T(8,128)(2,1)}), bf16[128,1024]{1,0:T(8,128)(2,1)}) %reduce-scatter.9.cloned.1.call-update) | async-done | bytes 262160 | tf_op jit(solution)/shard_map/reduce_scatter | solution.py:433
  474.9 68.4 %reduce-scatter.11.cloned.1.call-done = bf16[128,1024]{1,0:T(8,128)(2,1)} async-done(((bf16[1024,1024]{1,0:T(8,128)(2,1)}), bf16[128,1024]{1,0:T(8,128)(2,1)}) %reduce-scatter.11.cloned.1.call-update) | async-done | bytes 262160 | tf_op jit(solution)/shard_map/reduce_scatter | solution.py:432
  544.8 2.1 add_convert_fusion.2
  546.9 3.9 all-to-all-start.4
  550.9 2.5 reshape.567
  553.4 62.6 %all-gather.14.cloned.1.call-done = bf16[1024,1536]{0,1:T(8,128)(2,1)} async-done(((bf16[128,1536]{0,1:T(8,128)(2,1)}), bf16[1024,1536]{0,1:T(8,128)(2,1)}) %all-gather.14.cloned.1.call-update) | async-done | bytes 3145744 | tf_op jit(solution)/shard_map/all_gather | solution.py:357
  616.0 3.7 fusion.38
  623.7 57.2 %reduce-scatter.7.cloned.1.call-done = bf16[64,512]{1,0:T(8,128)(2,1)} async-done(((bf16[512,512]{1,0:T(8,128)(2,1)}), bf16[64,512]{1,0:T(8,128)(2,1)}) %reduce-scatter.7.cloned.1.call-update) | async-done | bytes 65552 | tf_op jit(solution)/shard_map/reduce_scatter | solution.py:430
  690.7 2.8 reshape.573
  694.4 2.5 fusion.13
  (357 shorter events, 103.2 us)
Async XLA Ops:
  7.2 156.5 %copy-start = (bf16[256,1024]{1,0:T(8,128)(2,1)S(1)}, bf16[256,1024]{1,0:T(8,128)(2,1)}, u32[]{:S(2)}) copy-start(bf16[256,1024]{1,0:T(8,128)(2,1)} %param.27) | copy-start | bytes 1572868
  7.2 91.1 %all-gather.8.cloned.1.call-start = ((), (), s32[]{:S(2)}) async-start(), calls=%async_computation.9 | async-start | bytes 8912896 | tf_op jit(solution)/shard_map/all_gather | solution.py:313
  9.8 49.8 %collective-permute-start.3 = (bf16[64,8,2,128]{3,1,2,0:T(8,128)(2,1)S(1)}, bf16[64,8,2,128]{3,1,2,0:T(8,128)(2,1)}, u32[]{:S(2)}, u32[]{:S(2)}) collective-permute-start(bf16[64,8,2,128]{3,1,2,0:T(8,128)(2,1)S(1)} %bitcast.221), channel_id=1, source_target_pairs={{0,1},{1,0},{2,3},{3,2},{4,5},{5,4},{6,7},{7,6},{8,9},{9,8},{10,11... | collective-permute-start | bytes 786440 | tf_op jit(solution)/shard_map/ppermute | solution.py:34
  12.9 49.6 %all-to-all-start = ((bf16[16,64,192]{2,1,0:T(8,128)(2,1)}), bf16[16,64,192]{2,1,0:T(8,128)(2,1)S(1)}, u32[]{:S(2)}, u32[]{:S(2)}) async-start(bf16[16,64,192]{2,1,0:T(8,128)(2,1)} %copy.206), calls=%async_computation | async-start | bytes 1048576 | tf_op jit(solution)/shard_map/all_to_all | solution.py:311
  19.9 139.2 %all-gather.10.cloned.1.call-start = ((), (), s32[]{:S(2)}) async-start(), calls=%async_computation.10 | async-start | bytes 1179648 | tf_op jit(solution)/shard_map/all_gather | solution.py:341
  20.6 171.8 %all-gather.12.cloned.1.call-start = ((), (), s32[]{:S(2)}) async-start(), calls=%async_computation.11 | async-start | bytes 2359296 | tf_op jit(solution)/shard_map/all_gather | solution.py:348
  61.9 180.5 %all-gather.16.cloned.1.call-start = ((), (), s32[]{:S(2)}) async-start(), calls=%async_computation.16 | async-start | bytes 2359296 | tf_op jit(solution)/shard_map/all_gather | solution.py:349
  163.7 3.0 collective-permute-start
  164.4 270.6 %reduce-scatter.13.cloned.1.call-start = ((), (), s32[]{:S(2)}) async-start(), calls=%async_computation.17 | async-start | bytes 626688
  169.0 30.6 %copy-start.21 = (bf16[256,1024]{1,0:T(8,128)(2,1)}, bf16[256,1024]{1,0:T(8,128)(2,1)S(1)}, u32[]{:S(2)}) copy-start(bf16[256,1024]{1,0:T(8,128)(2,1)S(1)} %fusion.19) | copy-start | bytes 1572868
  169.0 14.0 %collective-permute-start.1 = (bf16[256,1024]{1,0:T(8,128)(2,1)S(1)}, bf16[256,1024]{1,0:T(8,128)(2,1)S(1)}, u32[]{:S(2)}, u32[]{:S(2)}) collective-permute-start(bf16[256,1024]{1,0:T(8,128)(2,1)S(1)} %fusion.19), channel_id=1, source_target_pairs={{0,16},{16,0},{1,17},{17,1},{2,18},{18,2},{3,19},{19,3},{4,20},{20... | collective-permute-start | bytes 1572872 | tf_op jit(solution)/shard_map/ppermute | solution.py:38
  183.1 16.5 %copy-start.36 = (bf16[256,1024]{1,0:T(8,128)(2,1)}, bf16[256,1024]{1,0:T(8,128)(2,1)S(1)}, u32[]{:S(2)}) copy-start(bf16[256,1024]{1,0:T(8,128)(2,1)S(1)} %collective-permute-done.1) | copy-start | bytes 1572868
  184.2 8.3 %collective-permute-start.2 = (bf16[512,1024]{1,0:T(8,128)(2,1)}, bf16[512,1024]{1,0:T(8,128)(2,1)}, u32[]{:S(2)}, u32[]{:S(2)}) collective-permute-start(bf16[512,1024]{1,0:T(8,128)(2,1)} %pad_maximum_fusion.2), channel_id=1, source_target_pairs={{0,1},{1,0},{2,3},{3,2},{4,5},{5,4},{6,7},{7,6},{8,9},{9,8},{10,11... | collective-permute-start | bytes 3145736 | tf_op jit(solution)/shard_map/ppermute | solution.py:34
  184.2 15.4 %copy-start.52 = (f32[8,1,1,128]{3,2,1,0:T(1,128)}, f32[8,1,1,128]{3,2,1,0:T(1,128)S(1)}, u32[]{:S(2)}) copy-start(f32[8,1,1,128]{3,2,1,0:T(1,128)S(1)} %constant_dynamic-slice_fusion.5) | copy-start | bytes 12292
  249.6 4.5 collective-permute-start.4
  249.6 10.0 %copy-start.67 = (s32[2]{0:T(128)S(1)}, s32[2]{0:T(128)}, u32[]{:S(2)}) copy-start(s32[2]{0:T(128)} %len_ref.3) | copy-start | bytes 28
  249.6 11.0 %copy-start.48 = (bf16[2,128,128]{2,1,0:T(8,128)(2,1)S(1)}, bf16[2,128,128]{2,1,0:T(8,128)(2,1)}, u32[]{:S(2)}) copy-start(bf16[2,128,128]{2,1,0:T(8,128)(2,1)} %param.33) | copy-start | bytes 196612
  258.1 14.0 %collective-permute-start.5 = (bf16[256,1024]{1,0:T(8,128)(2,1)S(1)}, bf16[256,1024]{1,0:T(8,128)(2,1)S(1)}, u32[]{:S(2)}, u32[]{:S(2)}) collective-permute-start(bf16[256,1024]{1,0:T(8,128)(2,1)S(1)} %slice.256), channel_id=1, source_target_pairs={{0,16},{16,0},{1,17},{17,1},{2,18},{18,2},{3,19},{19,3},{4,20},{20... | collective-permute-start | bytes 1572872 | tf_op jit(solution)/shard_map/ppermute | solution.py:38
  259.7 14.4 %copy-start.34 = (bf16[16,64,128]{2,1,0:T(8,128)(2,1)}, bf16[16,64,128]{2,1,0:T(8,128)(2,1)S(1)}, u32[]{:S(2)}) copy-start(bf16[16,64,128]{2,1,0:T(8,128)(2,1)S(1)} %slice.205) | copy-start | bytes 786436
  260.7 13.4 %copy-start.66 = (bf16[2,128,1024]{2,1,0:T(8,128)(2,1)S(1)}, bf16[2,128,1024]{2,1,0:T(8,128)(2,1)}, u32[]{:S(2)}) copy-start(bf16[2,128,1024]{2,1,0:T(8,128)(2,1)} %param.32) | copy-start | bytes 1572868
  274.9 16.5 %copy-start.63 = (bf16[1,1024,1024]{2,1,0:T(8,128)(2,1)S(1)}, bf16[1,1024,1024]{2,1,0:T(8,128)(2,1)}, u32[]{:S(2)}) copy-start(bf16[1,1024,1024]{2,1,0:T(8,128)(2,1)} %all-gather.16.cloned.1.call-done) | copy-start | bytes 6291460
  274.9 16.5 %copy-start.69 = (f32[1024,1024]{1,0:T(8,128)S(1)}, f32[1024,1024]{1,0:T(8,128)}, u32[]{:S(2)}) copy-start(f32[1024,1024]{1,0:T(8,128)} %get-tuple-element.90) | copy-start | bytes 12582916
  275.4 22.6 %copy-start.25 = (bf16[256,1024]{1,0:T(8,128)(2,1)}, bf16[256,1024]{1,0:T(8,128)(2,1)S(1)}, u32[]{:S(2)}) copy-start(bf16[256,1024]{1,0:T(8,128)(2,1)S(1)} %get-tuple-element.43) | copy-start | bytes 1572868
  275.4 154.6 %copy-start.9 = (bf16[256,1024]{1,0:T(8,128)(2,1)}, bf16[256,1024]{1,0:T(8,128)(2,1)S(1)}, u32[]{:S(2)}) copy-start(bf16[256,1024]{1,0:T(8,128)(2,1)S(1)} %get-tuple-element.59) | copy-start | bytes 1572868
  275.4 16.0 %copy-start.53 = (f32[8,1,1,128]{3,2,1,0:T(1,128)S(1)}, f32[8,1,1,128]{3,2,1,0:T(1,128)}, u32[]{:S(2)}) copy-start(f32[8,1,1,128]{3,2,1,0:T(1,128)} %copy-done.52) | copy-start | bytes 12292
  275.4 13.2 %collective-permute-start.6 = (bf16[256,1024]{1,0:T(8,128)(2,1)S(1)}, bf16[256,1024]{1,0:T(8,128)(2,1)S(1)}, u32[]{:S(2)}, u32[]{:S(2)}) collective-permute-start(bf16[256,1024]{1,0:T(8,128)(2,1)S(1)} %get-tuple-element.43), channel_id=1, source_target_pairs={{0,16},{16,0},{1,17},{17,1},{2,18},{18,2},{3,19},{19,3},{4,20},{20... | collective-permute-start | bytes 1572872 | tf_op jit(solution)/shard_map/ppermute | solution.py:38
  288.6 2.7 collective-permute-start.7
  300.6 4.2 collective-permute-start.8
  307.7 14.3 %collective-permute-start.9 = (bf16[256,1024]{1,0:T(8,128)(2,1)}, bf16[256,1024]{1,0:T(8,128)(2,1)}, u32[]{:S(2)}, u32[]{:S(2)}) collective-permute-start(bf16[256,1024]{1,0:T(8,128)(2,1)} %slice.255), channel_id=1, source_target_pairs={{0,16},{16,0},{1,17},{17,1},{2,18},{18,2},{3,19},{19,3},{4,20},{20... | collective-permute-start | bytes 1572872 | tf_op jit(solution)/shard_map/ppermute | solution.py:38
  325.4 15.8 %copy-start.23 = (bf16[256,1024]{1,0:T(8,128)(2,1)}, bf16[256,1024]{1,0:T(8,128)(2,1)S(1)}, u32[]{:S(2)}) copy-start(bf16[256,1024]{1,0:T(8,128)(2,1)S(1)} %get-tuple-element.46) | copy-start | bytes 1572868
  326.6 147.1 %reduce-scatter.9.cloned.1.call-start = ((), (), s32[]{:S(2)}) async-start(), calls=%async_computation.14 | async-start | bytes 2359296 | tf_op jit(solution)/shard_map/reduce_scatter | solution.py:433
  332.3 211.0 %reduce-scatter.11.cloned.1.call-start = ((), (), s32[]{:S(2)}) async-start(), calls=%async_computation.15 | async-start | bytes 2359296 | tf_op jit(solution)/shard_map/reduce_scatter | solution.py:432
  339.2 2.0 collective-permute-start.10
  343.6 14.4 %copy-start.28 = (bf16[64,3072]{1,0:T(8,128)(2,1)S(1)}, bf16[64,3072]{1,0:T(8,128)(2,1)}, u32[]{:S(2)}) copy-start(bf16[64,3072]{1,0:T(8,128)(2,1)} %param.19) | copy-start | bytes 1179652
  345.8 21.6 %all-to-all-start.2 = ((bf16[8,2,2,128,64]{3,2,1,4,0:T(2,128)(2,1)}), bf16[8,2,2,128,64]{3,2,1,4,0:T(2,128)(2,1)S(1)}, u32[]{:S(2)}, u32[]{:S(2)}) async-start(bf16[8,2,2,128,64]{3,2,1,4,0:T(2,128)(2,1)} %bitcast.33), calls=%async_computation.2 | async-start | bytes 1048576 | tf_op jit(solution)/shard_map/all_to_all | solution.py:414
  349.3 266.7 %all-gather.14.cloned.1.call-start = ((), (), s32[]{:S(2)}) async-start(), calls=%async_computation.12 | async-start | bytes 3538944 | tf_op jit(solution)/shard_map/all_gather | solution.py:357
  360.2 2.9 collective-permute-start.11
  424.1 122.8 %all-to-all-start.3 = ((bf16[8,2,2,128,192]{3,2,1,4,0:T(2,128)(2,1)}), bf16[8,2,2,128,192]{3,2,1,4,0:T(2,128)(2,1)}, u32[]{:S(2)}, u32[]{:S(2)}) async-start(bf16[8,2,2,128,192]{3,2,1,4,0:T(2,128)(2,1)} %broadcast_select_fusion), calls=%async_computation.3 | async-start | bytes 3145728 | tf_op jit(solution)/shard_map/all_to_all | solution.py:528
  429.7 251.1 %reduce-scatter.7.cloned.1.call-start = ((), (), s32[]{:S(2)}) async-start(), calls=%async_computation.13 | async-start | bytes 589824 | tf_op jit(solution)/shard_map/reduce_scatter | solution.py:430
  435.8 3.8 collective-permute-start.16
  437.0 17.3 %collective-permute-start.14 = (bf16[512,512]{1,0:T(8,128)(2,1)}, bf16[512,512]{1,0:T(8,128)(2,1)}, u32[]{:S(2)}, u32[]{:S(2)}) collective-permute-start(bf16[512,512]{1,0:T(8,128)(2,1)} %convolution_convert_fusion.2), channel_id=1, source_target_pairs={{0,16},{16,0},{1,17},{17,1},{2,18},{18,2},{3,19},{19,3},{4,20},{20... | collective-permute-start | bytes 1572872 | tf_op jit(solution)/shard_map/ppermute | solution.py:38
  452.4 92.4 %collective-permute-start.13 = (bf16[16,80,192]{2,1,0:T(8,128)(2,1)S(1)}, bf16[16,80,192]{2,1,0:T(8,128)(2,1)}, u32[]{:S(2)}, u32[]{:S(2)}) collective-permute-start(bf16[16,80,192]{2,1,0:T(8,128)(2,1)S(1)} %pad_maximum_fusion.10), channel_id=1, source_target_pairs={{0,16},{16,0},{1,17},{17,1},{2,18},{18,2},{3,19},{19,3},{4,20},{20... | collective-permute-start | bytes 1474568 | tf_op jit(solution)/shard_map/ppermute | solution.py:38
  474.7 146.1 %collective-permute-start.17 = (bf16[64,8,128]{2,1,0:T(8,128)(2,1)S(1)}, bf16[64,8,128]{2,1,0:T(8,128)(2,1)S(1)}, u32[]{:S(2)}, u32[]{:S(2)}) collective-permute-start(bf16[64,8,128]{2,1,0:T(8,128)(2,1)S(1)} %get-tuple-element.68), channel_id=1, source_target_pairs={{0,1},{1,0},{2,3},{3,2},{4,5},{5,4},{6,7},{7,6},{8,9},{9,8},{10,11... | collective-permute-start | bytes 393224 | tf_op jit(solution)/shard_map/ppermute | solution.py:34
  543.3 79.1 %collective-permute-start.19 = (bf16[128,1024]{1,0:T(8,128)(2,1)}, bf16[128,1024]{1,0:T(8,128)(2,1)S(1)}, u32[]{:S(2)}, u32[]{:S(2)}) collective-permute-start(bf16[128,1024]{1,0:T(8,128)(2,1)} %reduce-scatter.11.cloned.1.call-done), channel_id=1, source_target_pairs={{0,16},{16,0},{1,17},{17,1},{2,18},{18,2},{3,19},{19,3},{4,20},{20... | collective-permute-start | bytes 786440 | tf_op jit(solution)/shard_map/ppermute | solution.py:38
  546.9 139.2 %all-to-all-start.4 = ((bf16[16,80,192]{2,1,0:T(8,128)(2,1)}), bf16[16,80,192]{2,1,0:T(8,128)(2,1)S(1)}, u32[]{:S(2)}, u32[]{:S(2)}) async-start(bf16[16,80,192]{2,1,0:T(8,128)(2,1)} %add_convert_fusion.2), calls=%async_computation.4 | async-start | bytes 1310720 | tf_op jit(solution)/shard_map/all_to_all | solution.py:520
  620.8 73.7 %collective-permute-start.12 = (f32[256,1024]{1,0:T(8,128)}, f32[256,1024]{1,0:T(8,128)}, u32[]{:S(2)}, u32[]{:S(2)}) collective-permute-start(f32[256,1024]{1,0:T(8,128)} %slice.213), channel_id=1, source_target_pairs={{0,1},{1,0},{2,3},{3,2},{4,5},{5,4},{6,7},{7,6},{8,9},{9,8},{10,11... | collective-permute-start | bytes 3145736 | tf_op jit(solution)/shard_map/ppermute | solution.py:34
  620.8 61.5 %collective-permute-start.18 = (bf16[64,8,2,128]{3,1,0,2:T(8,128)(2,1)S(1)}, bf16[64,8,2,128]{3,1,0,2:T(8,128)(2,1)S(1)}, u32[]{:S(2)}, u32[]{:S(2)}) collective-permute-start(bf16[64,8,2,128]{3,1,0,2:T(8,128)(2,1)S(1)} %maximum_select_fusion.5), channel_id=1, source_target_pairs={{0,16},{16,0},{1,17},{17,1},{2,18},{18,2},{3,19},{19,3},{4,20},{20... | collective-permute-start | bytes 786440 | tf_op jit(solution)/shard_map/ppermute | solution.py:38
  680.8 4.5 collective-permute-start.15
  (55 other events, 235.5 us)
Sparse Core Ops, SparseCore 0:
  10.2 88.0 all-gather.7
  100.5 38.9 all-gather.9
  142.1 50.3 all-gather.11
  195.0 47.2 all-gather.15
  326.7 56.6 reduce-scatter.12
  386.8 86.8 reduce-scatter.8
  477.2 66.0 reduce-scatter.10
  545.3 70.6 all-gather.13
  619.9 60.8 reduce-scatter.6
